TPU v7x, 512 devices: a whole 4x8x8 slice. The times are simulated.
512 devices in a mesh: wide: 64 (over y, z), narrow: 8 (over x, core).
Axes of the slice: x: 4, y: 8, z: 8, core: 2. Of those that a mesh axis runs over, the one named last changes fastest.
Arguments:
- right_side: bfloat16 [4, 1024, 512], P(None, 'wide'), may hold values from -6 to 6
- partial_in: float32 [8, 4, 1024, 512], P('narrow', None, 'wide'), may hold values from -6 to 6
- window_factor: bfloat16 [4, 1024, 4, 1024], P(None, 'wide', None, 'narrow'), may hold values from -0.09375 to 0.09375
- inverse_t: bfloat16 [4, 1024, 1024], P(None, 'wide', 'narrow'), as said below
- trailing_factor: bfloat16 [131072, 4, 1024], P('wide', None, 'narrow'), may hold values from -0.09375 to 0.09375
Outputs:
- solved: bfloat16 [4, 1024, 512], P(None, 'narrow')
- trailing: float32 [131072, 512], P(('wide', 'narrow'))
Inputs may be any that keep to these rules, and one draw needn't show every extreme that they name: inverse_t[k] is the transpose of the inverse of the k-th diagonal block of the lower-triangular factor: entry [k, j, i] is zero where j > i.
All inputs are finite; a program needn't handle non-finite values.
Results may differ from a plain program's by a relative error of at most 0.012.
Values may be sent and summed in bfloat16 or wider, within the bound.
No kernel may reach another device: no remote copies, remote signals or barrier semaphores. Data moves between devices by JAX's collectives and lax.ppermute only.
A program may use at most 64 MiB of HBM per device.

v0:
```python
import jax
import jax.numpy as jnp
from jax import lax
from jax.sharding import PartitionSpec as P


def per_device(right_side, partial_in, window_factor, inverse_t, trailing_factor):
    steps_count = right_side.shape[0]
    col_width = inverse_t.shape[2]
    rhs_width = right_side.shape[2]
    trail_rows = trailing_factor.shape[0]
    solved_list = []
    for block in range(steps_count):
        fanned = partial_in[0, block]
        for prior in range(block):
            fanned = fanned + jnp.dot(
                window_factor[block, :, prior, :],
                solved_list[prior],
                preferred_element_type=jnp.float32,
            )
        fanned = lax.psum(fanned, "narrow")
        residue = (right_side[block].astype(jnp.float32) - fanned).astype(jnp.bfloat16)
        solution = lax.dot_general(
            lax.all_gather(inverse_t[block], "wide", axis=0, tiled=True),
            lax.all_gather(residue, "wide", axis=0, tiled=True),
            (((0,), (0,)), ((), ())),
            preferred_element_type=jnp.float32,
        )
        solution = solution.astype(jnp.bfloat16)
        solved_list.append(solution)
    solved = jnp.stack(solved_list)
    flat_factor = trailing_factor.reshape(trail_rows, steps_count * col_width)
    flat_solved = solved.reshape(steps_count * col_width, rhs_width)
    trailing = lax.psum_scatter(
        jnp.dot(flat_factor, flat_solved, preferred_element_type=jnp.float32),
        "narrow",
        scatter_dimension=0,
        tiled=True,
    )
    return (solved, trailing)


def solution(mesh):
    placed = (
        P(None, "wide", None),
        P("narrow", None, "wide", None),
        P(None, "wide", None, "narrow"),
        P(None, "wide", "narrow"),
        P("wide", None, "narrow"),
    )
    return jax.shard_map(
        per_device,
        mesh=mesh,
        in_specs=placed,
        out_specs=(P(None, "narrow", None), P(("wide", "narrow"), None)),
        check_vma=False,
    )
```

profile of v0, /device:TPU:1, one launch (start us, length us, event | category | flops | bytes accessed | tf_op | source)
XLA Modules:
  0.0 481.9 jit_solution(5871402175136502424)
XLA Ops:
  7.2 0.9 slice_bitcast_fusion
  8.2 26.9 %psum.28 = f32[16,512]{1,0:T(8,128)S(1)} all-reduce(f32[16,512]{1,0:T(8,128)S(1)} %slice_bitcast_fusion), channel_id=1, replica_groups=mesh['wide'=64,'narrow'=8] {'narrow'}, use_global_device_ids=true, to_apply=%region_0.0 | all-reduce | flops 8192 | bytes 65536 | tf_op jit(solution)/shard_map/psum | solution.py:21
  35.0 1.3 fusion.15
  37.2 43.0 %all-gather = bf16[1,1024,128]{2,1,0:T(8,128)(2,1)S(1)} all-gather(bf16[1,16,128]{2,1,0:T(8,128)(2,1)S(1)} %get-tuple-element.14), channel_id=2, replica_groups=mesh['wide'=64,'narrow'=8] {'wide'}, dimensions={1}, use_global_device_ids=true | all-gather | bytes 266240 | tf_op jit(solution)/shard_map/all_gather | solution.py:24
  80.2 0.9 fusion.16
  81.1 34.6 %all-gather.9.cloned.1.call-done = bf16[1024,512]{1,0:T(8,128)(2,1)} async-done(((bf16[16,512]{1,0:T(8,128)(2,1)}), bf16[1024,512]{1,0:T(8,128)(2,1)}) %all-gather.9.cloned.1.call-update) | async-done | bytes 1048592 | tf_op jit(solution)/shard_map/all_gather | solution.py:25
  115.6 1.7 convolution_convert_fusion.3
  117.3 0.9 fusion.7
  118.2 25.6 %psum.29 = f32[16,512]{1,0:T(8,128)S(1)} all-reduce(f32[16,512]{1,0:T(8,128)S(1)} %fusion.7), channel_id=1, replica_groups=mesh['wide'=64,'narrow'=8] {'narrow'}, use_global_device_ids=true, to_apply=%region_1.0 | all-reduce | flops 8192 | bytes 65536 | tf_op jit(solution)/shard_map/psum | solution.py:21
  144.5 36.7 %all-gather.1 = bf16[1,1024,128]{2,1,0:T(8,128)(2,1)S(1)} all-gather(bf16[1,16,128]{2,1,0:T(8,128)(2,1)S(1)} %get-tuple-element.13), channel_id=3, replica_groups=mesh['wide'=64,'narrow'=8] {'wide'}, dimensions={1}, use_global_device_ids=true | all-gather | bytes 266240 | tf_op jit(solution)/shard_map/all_gather | solution.py:24
  181.4 37.9 %all-gather.11.cloned.1.call-done = bf16[1024,512]{1,0:T(8,128)(2,1)} async-done(((bf16[16,512]{1,0:T(8,128)(2,1)}), bf16[1024,512]{1,0:T(8,128)(2,1)}) %all-gather.11.cloned.1.call-update) | async-done | bytes 1048592 | tf_op jit(solution)/shard_map/all_gather | solution.py:25
  219.3 1.7 convolution_convert_fusion.2
  221.1 25.6 %psum.30 = f32[16,512]{1,0:T(8,128)S(1)} all-reduce(f32[16,512]{1,0:T(8,128)S(1)} %fusion.5), channel_id=1, replica_groups=mesh['wide'=64,'narrow'=8] {'narrow'}, use_global_device_ids=true, to_apply=%region_2.0 | all-reduce | flops 8192 | bytes 65536 | tf_op jit(solution)/shard_map/psum | solution.py:21
  247.4 36.7 %all-gather.2 = bf16[1,1024,128]{2,1,0:T(8,128)(2,1)S(1)} all-gather(bf16[1,16,128]{2,1,0:T(8,128)(2,1)S(1)} %get-tuple-element.15), channel_id=4, replica_groups=mesh['wide'=64,'narrow'=8] {'wide'}, dimensions={1}, use_global_device_ids=true | all-gather | bytes 266240 | tf_op jit(solution)/shard_map/all_gather | solution.py:24
  284.4 37.8 %all-gather.13.cloned.1.call-done = bf16[1024,512]{1,0:T(8,128)(2,1)} async-done(((bf16[16,512]{1,0:T(8,128)(2,1)}), bf16[1024,512]{1,0:T(8,128)(2,1)}) %all-gather.13.cloned.1.call-update) | async-done | bytes 1048592 | tf_op jit(solution)/shard_map/all_gather | solution.py:25
  322.3 1.7 convolution_convert_fusion.1
  324.1 25.6 %psum.31 = f32[16,512]{1,0:T(8,128)S(1)} all-reduce(f32[16,512]{1,0:T(8,128)S(1)} %fusion.2), channel_id=1, replica_groups=mesh['wide'=64,'narrow'=8] {'narrow'}, use_global_device_ids=true, to_apply=%region_3.0 | all-reduce | flops 8192 | bytes 65536 | tf_op jit(solution)/shard_map/psum | solution.py:21
  350.4 36.3 %all-gather.3 = bf16[1,1024,128]{2,1,0:T(8,128)(2,1)S(1)} all-gather(bf16[1,16,128]{2,1,0:T(8,128)(2,1)S(1)} %get-tuple-element.12), channel_id=5, replica_groups=mesh['wide'=64,'narrow'=8] {'wide'}, dimensions={1}, use_global_device_ids=true | all-gather | bytes 266240 | tf_op jit(solution)/shard_map/all_gather | solution.py:24
  386.7 38.5 %all-gather.15.cloned.1.call-done = bf16[1024,512]{1,0:T(8,128)(2,1)} async-done(((bf16[16,512]{1,0:T(8,128)(2,1)}), bf16[1024,512]{1,0:T(8,128)(2,1)}) %all-gather.15.cloned.1.call-update) | async-done | bytes 1048592 | tf_op jit(solution)/shard_map/all_gather | solution.py:25
  425.2 1.7 fusion.1
  426.9 3.2 convolution_bitcast_fusion
  430.2 1.0 copy.17
  431.3 42.1 %reduce-scatter.2.cloned.1.call-done = f32[256,512]{0,1:T(8,128)} async-done(((f32[2048,512]{0,1:T(8,128)}), f32[256,512]{0,1:T(8,128)}) %reduce-scatter.2.cloned.1.call-update) | async-done | bytes 524304 | tf_op jit(solution)/shard_map/reduce_scatter | solution.py:34
  473.4 2.0 copy.18
  (26 shorter events, 3.7 us)
Async XLA Ops:
  7.2 419.7 %copy-start = (bf16[2048,4,128]{2,1,0:T(4,128)(2,1)S(1)}, bf16[2048,4,128]{2,1,0:T(4,128)(2,1)}, u32[]{:S(2)}) copy-start(bf16[2048,4,128]{2,1,0:T(4,128)(2,1)} %param.9) | copy-start | bytes 6291460
  7.2 174.1 %copy-start.1 = (f32[1,4,16,512]{3,2,1,0:T(8,128)S(1)}, f32[1,4,16,512]{3,2,1,0:T(8,128)}, u32[]{:S(2)}) copy-start(f32[1,4,16,512]{3,2,1,0:T(8,128)} %param.6) | copy-start | bytes 393220
  7.2 136.6 %copy-start.2 = (bf16[4,16,512]{2,1,0:T(8,128)(2,1)S(1)}, bf16[4,16,512]{2,1,0:T(8,128)(2,1)}, u32[]{:S(2)}) copy-start(bf16[4,16,512]{2,1,0:T(8,128)(2,1)} %param.5) | copy-start | bytes 196612
  7.2 108.4 %all-gather.9.cloned.1.call-start = ((), (), s32[]{:S(2)}) async-start(), calls=%async_computation.1 | async-start | bytes 1064960 | tf_op jit(solution)/shard_map/all_gather | solution.py:25
  36.4 182.9 %all-gather.11.cloned.1.call-start = ((), (), s32[]{:S(2)}) async-start(), calls=%async_computation.2 | async-start | bytes 1064960 | tf_op jit(solution)/shard_map/all_gather | solution.py:25
  144.5 177.8 %all-gather.13.cloned.1.call-start = ((), (), s32[]{:S(2)}) async-start(), calls=%async_computation.3 | async-start | bytes 1064960 | tf_op jit(solution)/shard_map/all_gather | solution.py:25
  247.4 177.8 %all-gather.15.cloned.1.call-start = ((), (), s32[]{:S(2)}) async-start(), calls=%async_computation.4 | async-start | bytes 1064960 | tf_op jit(solution)/shard_map/all_gather | solution.py:25
  350.3 123.0 %reduce-scatter.2.cloned.1.call-start = ((), (), s32[]{:S(2)}) async-start(), calls=%async_computation.5 | async-start | bytes 4718592 | tf_op jit(solution)/shard_map/reduce_scatter | solution.py:34
Sparse Core Ops, SparseCore 0:
  36.5 79.0 all-gather.8
  144.6 74.6 all-gather.10
  247.5 74.7 all-gather.12
  350.4 74.6 all-gather.14
  430.3 43.0 reduce-scatter.1
where the time goes:
time: 484 us; the launch traced here: 482 us
  blocking collectives  256 us (53%)
  waiting for transfers between devices  191 us (39%)
  between operations  13.9 us (3%)
  matrix products  11.7 us (2%)
  local copies, waits for them, and re-layouts  5.6 us (1%)
    all_gather x4, blocking collectives, per_device(): lax.all_gather(inverse_t[block], 'wide', axis=0, tiled=True)  153 us
    all_gather x4, waiting for transfers between devices, per_device(): lax.all_gather(residue, 'wide', axis=0, tiled=True)  149 us
    psum x4, blocking collectives, per_device(): fanned = lax.psum(fanned, 'narrow')  104 us
    reduce_scatter x1, waiting for transfers between devices, per_device(): lax.psum_scatter(jnp.dot(flat_factor, flat_solved, preferred_element_type...  42.1 us
  transfers between devices with their start and end apart: 5, of which 5 were waited for; matrix products, arithmetic and copies ran while one was open for 1% of the time, Pallas kernels for 0%

commit v1 on v0

v1 whole, which is shorter than its diff:
```python
import jax
import jax.numpy as jnp
from jax import lax
from jax.sharding import Mesh
from jax.sharding import PartitionSpec as P

F32 = jnp.float32
BF16 = jnp.bfloat16
NARROW = ("x", "core")
NUM_Y, NUM_Z, NUM_X, NUM_CORE = 8, 8, 4, 2
NUM_NARROW = NUM_X * NUM_CORE


def spread(value, axis, count):
    copies = jnp.broadcast_to(value[None], (count,) + value.shape)
    return lax.all_to_all(copies, axis, 0, 0, tiled=True)


def per_device(right_side, partial_in, window_factor, inverse_t, trailing_factor):
    steps, rows, rhs = right_side.shape
    cols = inverse_t.shape[2]
    part = rhs // NUM_Y
    slab = rows * NUM_Y
    trail_rows = trailing_factor.shape[0]

    first = (lax.axis_index(NARROW) == 0).astype(F32)
    terms = partial_in[0] - right_side.astype(F32) * first
    terms = terms.reshape(steps, rows, NUM_Y, part).transpose(2, 0, 1, 3)
    terms = lax.all_to_all(terms, "y", 0, 0, tiled=True)
    terms = terms.transpose(1, 3, 0, 2).reshape(steps, part, slab)

    pairs = [(block, prior) for block in range(steps) for prior in range(block)]
    pieces = [window_factor[block, :, prior, :] for block, prior in pairs]
    pieces += [inverse_t[block] for block in range(steps)]
    pieces = spread(jnp.stack(pieces), "y", NUM_Y)
    pieces = pieces.transpose(1, 0, 2, 3).reshape(-1, slab, cols)
    window = {pair: pieces[i] for i, pair in enumerate(pairs)}
    inverse = [pieces[len(pairs) + block] for block in range(steps)]

    solved_t = []
    for block in range(steps):
        fanned = terms[block]
        for prior in range(block):
            fanned = fanned + lax.dot_general(
                solved_t[prior], window[block, prior], (((1,), (1,)), ((), ())),
                preferred_element_type=F32,
            )
        fanned = spread(fanned, NARROW, NUM_NARROW).sum(0)
        residue = (-fanned).astype(BF16)
        share = jnp.dot(residue, inverse[block], preferred_element_type=F32)
        share = spread(share, "z", NUM_Z).sum(0)
        solved_t.append(share.astype(BF16))

    every = spread(jnp.stack(solved_t), "y", NUM_Y)
    every = every.transpose(1, 0, 2, 3).reshape(steps, rhs, cols)
    solved = every.transpose(0, 2, 1)

    trailing = jnp.zeros((trail_rows, rhs), F32)
    flat_factor = trailing_factor.reshape(trail_rows, steps * cols)
    flat_solved = solved.reshape(steps * cols, rhs)
    trailing = jnp.dot(flat_factor, flat_solved, preferred_element_type=F32)

    own = trail_rows // NUM_NARROW
    trailing = trailing.reshape(NUM_X, NUM_CORE, own, rhs)
    core = lax.axis_index("core")
    away = lax.dynamic_index_in_dim(trailing, 1 - core, 1, keepdims=False)
    kept = lax.dynamic_index_in_dim(trailing, core, 1, keepdims=False)
    back = lax.ppermute(away.astype(BF16), "core", [(0, 1), (1, 0)])
    pair_sum = (kept + back.astype(F32)).astype(BF16)
    pair_sum = lax.all_to_all(pair_sum, "x", 0, 0, tiled=True)
    trailing = pair_sum.astype(F32).sum(0)
    return (solved, trailing)


def solution(mesh):
    grid = Mesh(
        mesh.devices.reshape(NUM_Y, NUM_Z, NUM_X, NUM_CORE), ("y", "z", "x", "core")
    )
    wide = ("y", "z")
    placed = (
        P(None, wide, None),
        P(NARROW, None, wide, None),
        P(None, wide, None, NARROW),
        P(None, wide, NARROW),
        P(wide, None, NARROW),
    )
    return jax.shard_map(
        per_device,
        mesh=grid,
        in_specs=placed,
        out_specs=(P(None, NARROW, None), P(wide + NARROW, None)),
        check_vma=False,
    )
```

time: 484 us -> 233 us (0.48)
  blocking collectives: 256 us -> 49.1 us
  waiting for transfers between devices: 191 us -> 83.8 us
  starting transfers between devices: 0.21 us -> 47.2 us
  local copies, waits for them, and re-layouts: 5.6 us -> 37.8 us
  between operations: 13.9 us -> 0.87 us
  matrix products: 11.7 us -> 4.61 us
    all_gather x4 -> x0, blocking collectives: 153 us -> none  [per_device(): lax.all_gather(inverse_t[block], 'wide', axis=0, tiled=True)]
    all_gather x4 -> x0, waiting for transfers between devices: 149 us -> none  [per_device(): lax.all_gather(residue, 'wide', axis=0, tiled=True)]
    psum x4 -> x0, blocking collectives: 104 us -> none  [per_device(): fanned = lax.psum(fanned, 'narrow')]
    all_to_all x0 -> x8, waiting for transfers between devices: none -> 83.8 us  [the longest x6 62.5 us: spread(): return lax.all_to_all(copies, axis, 0, 0, tiled=True)]
    all_to_all x0 -> x4, blocking collectives: none -> 49.1 us  [spread(): return lax.all_to_all(copies, axis, 0, 0, tiled=True)]
    reduce_scatter x1 -> x0, waiting for transfers between devices: 42.1 us -> none  [per_device(): lax.psum_scatter(jnp.dot(flat_factor, flat_solved, preferred_element_type...]
    all_to_all x0 -> x8, starting transfers between devices: none -> 41.9 us  [the longest x6 30.1 us: spread(): return lax.all_to_all(copies, axis, 0, 0, tiled=True)]
    dynamic_slice x0 -> x3, local copies, waits for them, and re-layouts: none -> 16.8 us  [the longest x2 11.4 us: per_device(): kept = lax.dynamic_index_in_dim(trailing, core, 1, keepdims=False)]
  transfers between devices with their start and end apart: 5 -> 9, of which waited for: 5 -> 8; matrix products, arithmetic and copies ran while one was open for 1% -> 6% of each run, Pallas kernels for 0% -> 0%
where the time goes in v1:
time: 233 us; the launch traced here: 231 us
  waiting for transfers between devices  83.8 us (36%)
  blocking collectives  49.1 us (21%)
  starting transfers between devices  47.2 us (20%)
  local copies, waits for them, and re-layouts  37.8 us (16%)
  other arithmetic  7.59 us (3%)
  matrix products  4.61 us (2%)
    all_to_all x6, waiting for transfers between devices, spread(): return lax.all_to_all(copies, axis, 0, 0, tiled=True)  62.5 us
    all_to_all x4, blocking collectives, spread(): return lax.all_to_all(copies, axis, 0, 0, tiled=True)  49.1 us
    all_to_all x6, starting transfers between devices, spread(): return lax.all_to_all(copies, axis, 0, 0, tiled=True)  30.1 us
    all_to_all x1, waiting for transfers between devices, per_device(): pair_sum = lax.all_to_all(pair_sum, 'x', 0, 0, tiled=True)  14.2 us
    dynamic_slice x2, local copies, waits for them, and re-layouts, per_device(): kept = lax.dynamic_index_in_dim(trailing, core, 1, keepdims=False)  11.4 us
    unnamed x14, local copies, waits for them, and re-layouts  7.83 us
    all_to_all x1, starting transfers between devices, per_device(): terms = lax.all_to_all(terms, 'y', 0, 0, tiled=True)  7.64 us
    all_to_all x1, waiting for transfers between devices, per_device(): terms = lax.all_to_all(terms, 'y', 0, 0, tiled=True)  7.09 us
  transfers between devices with their start and end apart: 9, of which 8 were waited for; matrix products, arithmetic and copies ran while one was open for 6% of the time, Pallas kernels for 0%

profile of v1, /device:TPU:1, one launch (start us, length us, event | category | flops | bytes accessed | tf_op | source)
XLA Modules:
  0.0 231.0 jit_solution(1344628116994190797)
XLA Ops:
  2.7 7.6 %all-to-all-start = ((f32[8,1,4096]{2,1,0:T(1,128)}), f32[8,1,4096]{2,1,0:T(1,128)S(1)}, u32[]{:S(2)}, u32[]{:S(2)}) async-start(f32[8,1,4096]{2,1,0:T(1,128)} %reshape.91), calls=%async_computation | async-start | bytes 262144 | tf_op jit(solution)/shard_map/all_to_all | solution.py:29
  11.3 7.1 %all-to-all-done = f32[8,1,4096]{2,1,0:T(1,128)S(1)} async-done(((f32[8,1,4096]{2,1,0:T(1,128)}), f32[8,1,4096]{2,1,0:T(1,128)S(1)}, u32[]{:S(2)}, u32[]{:S(2)}) %all-to-all-start) | async-done | bytes 131104 | tf_op jit(solution)/shard_map/all_to_all | solution.py:29
  20.8 6.9 %all-to-all-start.1 = ((f32[8,64,128]{2,1,0:T(8,128)}), f32[8,64,128]{2,1,0:T(8,128)S(1)}, u32[]{:S(2)}, u32[]{:S(2)}) async-start(f32[8,64,128]{2,1,0:T(8,128)} %broadcast_in_dim.23), calls=%async_computation.1 | async-start | bytes 524288 | tf_op jit(solution)/shard_map/all_to_all | solution.py:16
  27.7 6.5 %all-to-all-done.1 = f32[8,64,128]{2,1,0:T(8,128)S(1)} async-done(((f32[8,64,128]{2,1,0:T(8,128)}), f32[8,64,128]{2,1,0:T(8,128)S(1)}, u32[]{:S(2)}, u32[]{:S(2)}) %all-to-all-start.1) | async-done | bytes 262176 | tf_op jit(solution)/shard_map/all_to_all | solution.py:16
  34.9 3.4 %all-to-all-start.2 = ((bf16[8,10,16,128]{3,2,1,0:T(8,128)(2,1)}), bf16[8,10,16,128]{3,2,1,0:T(8,128)(2,1)S(1)}, u32[]{:S(2)}, u32[]{:S(2)}) async-start(bf16[8,10,16,128]{3,2,1,0:T(8,128)(2,1)} %broadcast_in_dim.24), calls=%async_computation.2 | async-start | bytes 655360 | tf_op jit(solution)/shard_map/all_to_all | solution.py:16
  38.4 11.8 %all-to-all-done.2 = bf16[8,10,16,128]{3,2,1,0:T(8,128)(2,1)S(1)} async-done(((bf16[8,10,16,128]{3,2,1,0:T(8,128)(2,1)}), bf16[8,10,16,128]{3,2,1,0:T(8,128)(2,1)S(1)}, u32[]{:S(2)}, u32[]{:S(2)}) %all-to-all-start.2) | async-done | bytes 327712 | tf_op jit(solution)/shard_map/all_to_all | solution.py:16
  51.1 9.5 %all-to-all-start.3 = ((f32[8,64,128]{2,1,0:T(8,128)}), f32[8,64,128]{2,1,0:T(8,128)S(1)}, u32[]{:S(2)}, u32[]{:S(2)}) async-start(f32[8,64,128]{2,1,0:T(8,128)} %broadcast_in_dim.25), calls=%async_computation.3 | async-start | bytes 524288 | tf_op jit(solution)/shard_map/all_to_all | solution.py:16
  60.6 9.3 %all-to-all-done.3 = f32[8,64,128]{2,1,0:T(8,128)S(1)} async-done(((f32[8,64,128]{2,1,0:T(8,128)}), f32[8,64,128]{2,1,0:T(8,128)S(1)}, u32[]{:S(2)}, u32[]{:S(2)}) %all-to-all-start.3) | async-done | bytes 262176 | tf_op jit(solution)/shard_map/all_to_all | solution.py:16
  70.2 13.6 %all_to_all.60 = f32[8,64,128]{2,1,0:T(8,128)S(1)} all-to-all(f32[8,64,128]{2,1,0:T(8,128)S(1)} %broadcast_in_dim.26), channel_id=1, replica_groups=mesh['y'=8,'z'=8,'x'=4,'core'=2] {'x','core'}, dimensions={0} | all-to-all | bytes 524288 | tf_op jit(solution)/shard_map/all_to_all | solution.py:16
  88.3 10.0 %all-to-all-done.5 = f32[8,64,128]{2,1,0:T(8,128)S(1)} async-done(((f32[8,64,128]{2,1,0:T(8,128)}), f32[8,64,128]{2,1,0:T(8,128)S(1)}, u32[]{:S(2)}, u32[]{:S(2)}) %all-to-all-start.5) | async-done | bytes 262176 | tf_op jit(solution)/shard_map/all_to_all | solution.py:16
  98.5 11.4 %all_to_all.61 = f32[8,64,128]{2,1,0:T(8,128)S(1)} all-to-all(f32[8,64,128]{2,1,0:T(8,128)S(1)} %broadcast_in_dim.28), channel_id=1, replica_groups=mesh['y'=8,'z'=8,'x'=4,'core'=2] {'x','core'}, dimensions={0} | all-to-all | bytes 524288 | tf_op jit(solution)/shard_map/all_to_all | solution.py:16
  114.6 9.9 %all-to-all-done.7 = f32[8,64,128]{2,1,0:T(8,128)S(1)} async-done(((f32[8,64,128]{2,1,0:T(8,128)}), f32[8,64,128]{2,1,0:T(8,128)S(1)}, u32[]{:S(2)}, u32[]{:S(2)}) %all-to-all-start.7) | async-done | bytes 262176 | tf_op jit(solution)/shard_map/all_to_all | solution.py:16
  124.6 11.4 %all_to_all.62 = f32[8,64,128]{2,1,0:T(8,128)S(1)} all-to-all(f32[8,64,128]{2,1,0:T(8,128)S(1)} %broadcast_in_dim.30), channel_id=1, replica_groups=mesh['y'=8,'z'=8,'x'=4,'core'=2] {'x','core'}, dimensions={0} | all-to-all | bytes 524288 | tf_op jit(solution)/shard_map/all_to_all | solution.py:16
  136.2 12.7 %all_to_all.63 = f32[8,64,128]{2,1,0:T(8,128)S(1)} all-to-all(f32[8,64,128]{2,1,0:T(8,128)S(1)} %broadcast_in_dim.31), channel_id=1, replica_groups=mesh['y'=8,'z'=8,'x'=4,'core'=2] {'z'}, dimensions={0} | all-to-all | bytes 524288 | tf_op jit(solution)/shard_map/all_to_all | solution.py:16
  149.9 3.5 %all-to-all-start.10 = ((bf16[8,4,64,128]{3,2,1,0:T(8,128)(2,1)}), bf16[8,4,64,128]{3,2,1,0:T(8,128)(2,1)S(1)}, u32[]{:S(2)}, u32[]{:S(2)}) async-start(bf16[8,4,64,128]{3,2,1,0:T(8,128)(2,1)} %broadcast_in_dim.32), calls=%async_computation.10 | async-start | bytes 1048576 | tf_op jit(solution)/shard_map/all_to_all | solution.py:16
  153.4 15.0 %all-to-all-done.10 = bf16[8,4,64,128]{3,2,1,0:T(8,128)(2,1)S(1)} async-done(((bf16[8,4,64,128]{3,2,1,0:T(8,128)(2,1)}), bf16[8,4,64,128]{3,2,1,0:T(8,128)(2,1)S(1)}, u32[]{:S(2)}, u32[]{:S(2)}) %all-to-all-start.10) | async-done | bytes 524320 | tf_op jit(solution)/shard_map/all_to_all | solution.py:16
  171.7 6.6 %reshape.89 = f32[4,2,256,512]{2,1,0,3:T(2,128)} reshape(f32[2048,512]{0,1:T(8,128)} %convolution_bitcast_fusion) | data formatting | bytes 8388608 | tf_op jit(solution)/shard_map/reshape | solution.py:64
  178.3 5.4 %constant_dynamic-slice_fusion = bf16[4,1,256,512]{2,1,0,3:T(2,128)(2,1)} fusion(f32[4,2,256,512]{2,1,0,3:T(2,128)} %reshape.89, s32[]{:T(128)S(6)} %select_n.8), kind=kLoop, calls=%fused_computation.38 | loop fusion | bytes 2097156 | tf_op jit(solution)/shard_map/jit(dynamic_index_in_dim)/dynamic_slice | solution.py:66
  183.7 5.8 %copy.83 = bf16[4,1,256,512]{3,2,0,1:T(8,128)(2,1)} copy(bf16[4,1,256,512]{2,1,0,3:T(2,128)(2,1)} %constant_dynamic-slice_fusion) | data formatting | bytes 2097152
  189.5 5.2 %collective-permute-start = (bf16[4,256,512]{2,1,0:T(8,128)(2,1)}, bf16[4,256,512]{2,1,0:T(8,128)(2,1)}, u32[]{:S(2)}, u32[]{:S(2)}) collective-permute-start(bf16[4,256,512]{2,1,0:T(8,128)(2,1)} %bitcast.91), channel_id=1, source_target_pairs={{0,1},{1,0},{2,3},{3,2},{4,5},{5,4},{6,7},{7,6},{8,9},{9,8},{10,11... | collective-permute-start | bytes 3145736 | tf_op jit(solution)/shard_map/ppermute | solution.py:68
  194.8 5.3 %constant_dynamic-slice_fusion.1 = f32[4,1,256,512]{2,1,0,3:T(1,128)} fusion(f32[4,2,256,512]{2,1,0,3:T(2,128)} %reshape.89, s32[]{:T(128)S(6)} %select_n.7), kind=kLoop, calls=%fused_computation.39 | loop fusion | bytes 4194308 | tf_op jit(solution)/shard_map/jit(dynamic_index_in_dim)/dynamic_slice | solution.py:67
  200.1 6.0 %copy.74 = f32[4,1,256,512]{3,2,0,1:T(8,128)} copy(f32[4,1,256,512]{2,1,0,3:T(1,128)} %constant_dynamic-slice_fusion.1) | data formatting | bytes 4194304 | tf_op jit(solution)/shard_map/jit(dynamic_index_in_dim)/dynamic_slice | solution.py:67
  209.3 4.2 %all-to-all-start.11 = ((bf16[4,256,512]{2,1,0:T(8,128)(2,1)}), bf16[4,256,512]{2,1,0:T(8,128)(2,1)}, u32[]{:S(2)}, u32[]{:S(2)}) async-start(bf16[4,256,512]{2,1,0:T(8,128)(2,1)} %fusion), calls=%async_computation.11 | async-start | bytes 2097152 | tf_op jit(solution)/shard_map/all_to_all | solution.py:70
  214.6 14.2 %all-to-all-done.11 = bf16[4,256,512]{2,1,0:T(8,128)(2,1)} async-done(((bf16[4,256,512]{2,1,0:T(8,128)(2,1)}), bf16[4,256,512]{2,1,0:T(8,128)(2,1)}, u32[]{:S(2)}, u32[]{:S(2)}) %all-to-all-start.11) | async-done | bytes 1048608 | tf_op jit(solution)/shard_map/all_to_all | solution.py:70
  (62 shorter events, 27.7 us)
Async XLA Ops:
  0.6 167.8 %copy-start = (bf16[2048,4,128]{2,1,0:T(4,128)(2,1)S(1)}, bf16[2048,4,128]{2,1,0:T(4,128)(2,1)}, u32[]{:S(2)}) copy-start(bf16[2048,4,128]{2,1,0:T(4,128)(2,1)} %param.9) | copy-start | bytes 6291460
  0.7 27.0 %copy-start.1 = (bf16[4,16,128]{2,1,0:T(8,128)(2,1)S(1)}, bf16[4,16,128]{2,1,0:T(8,128)(2,1)}, u32[]{:S(2)}) copy-start(bf16[4,16,128]{2,1,0:T(8,128)(2,1)} %param.8) | copy-start | bytes 49156
  2.7 15.7 %all-to-all-start = ((f32[8,1,4096]{2,1,0:T(1,128)}), f32[8,1,4096]{2,1,0:T(1,128)S(1)}, u32[]{:S(2)}, u32[]{:S(2)}) async-start(f32[8,1,4096]{2,1,0:T(1,128)} %reshape.91), calls=%async_computation | async-start | bytes 262144 | tf_op jit(solution)/shard_map/all_to_all | solution.py:29
  20.8 13.4 %all-to-all-start.1 = ((f32[8,64,128]{2,1,0:T(8,128)}), f32[8,64,128]{2,1,0:T(8,128)S(1)}, u32[]{:S(2)}, u32[]{:S(2)}) async-start(f32[8,64,128]{2,1,0:T(8,128)} %broadcast_in_dim.23), calls=%async_computation.1 | async-start | bytes 524288 | tf_op jit(solution)/shard_map/all_to_all | solution.py:16
  34.9 15.3 %all-to-all-start.2 = ((bf16[8,10,16,128]{3,2,1,0:T(8,128)(2,1)}), bf16[8,10,16,128]{3,2,1,0:T(8,128)(2,1)S(1)}, u32[]{:S(2)}, u32[]{:S(2)}) async-start(bf16[8,10,16,128]{3,2,1,0:T(8,128)(2,1)} %broadcast_in_dim.24), calls=%async_computation.2 | async-start | bytes 655360 | tf_op jit(solution)/shard_map/all_to_all | solution.py:16
  51.1 18.9 %all-to-all-start.3 = ((f32[8,64,128]{2,1,0:T(8,128)}), f32[8,64,128]{2,1,0:T(8,128)S(1)}, u32[]{:S(2)}, u32[]{:S(2)}) async-start(f32[8,64,128]{2,1,0:T(8,128)} %broadcast_in_dim.25), calls=%async_computation.3 | async-start | bytes 524288 | tf_op jit(solution)/shard_map/all_to_all | solution.py:16
  84.7 13.6 %all-to-all-start.5 = ((f32[8,64,128]{2,1,0:T(8,128)}), f32[8,64,128]{2,1,0:T(8,128)S(1)}, u32[]{:S(2)}, u32[]{:S(2)}) async-start(f32[8,64,128]{2,1,0:T(8,128)} %broadcast_in_dim.27), calls=%async_computation.5 | async-start | bytes 524288 | tf_op jit(solution)/shard_map/all_to_all | solution.py:16
  110.8 13.6 %all-to-all-start.7 = ((f32[8,64,128]{2,1,0:T(8,128)}), f32[8,64,128]{2,1,0:T(8,128)S(1)}, u32[]{:S(2)}, u32[]{:S(2)}) async-start(f32[8,64,128]{2,1,0:T(8,128)} %broadcast_in_dim.29), calls=%async_computation.7 | async-start | bytes 524288 | tf_op jit(solution)/shard_map/all_to_all | solution.py:16
  149.9 18.5 %all-to-all-start.10 = ((bf16[8,4,64,128]{3,2,1,0:T(8,128)(2,1)}), bf16[8,4,64,128]{3,2,1,0:T(8,128)(2,1)S(1)}, u32[]{:S(2)}, u32[]{:S(2)}) async-start(bf16[8,4,64,128]{3,2,1,0:T(8,128)(2,1)} %broadcast_in_dim.32), calls=%async_computation.10 | async-start | bytes 1048576 | tf_op jit(solution)/shard_map/all_to_all | solution.py:16
  189.5 16.6 %collective-permute-start = (bf16[4,256,512]{2,1,0:T(8,128)(2,1)}, bf16[4,256,512]{2,1,0:T(8,128)(2,1)}, u32[]{:S(2)}, u32[]{:S(2)}) collective-permute-start(bf16[4,256,512]{2,1,0:T(8,128)(2,1)} %bitcast.91), channel_id=1, source_target_pairs={{0,1},{1,0},{2,3},{3,2},{4,5},{5,4},{6,7},{7,6},{8,9},{9,8},{10,11... | collective-permute-start | bytes 3145736 | tf_op jit(solution)/shard_map/ppermute | solution.py:68
  209.3 19.5 %all-to-all-start.11 = ((bf16[4,256,512]{2,1,0:T(8,128)(2,1)}), bf16[4,256,512]{2,1,0:T(8,128)(2,1)}, u32[]{:S(2)}, u32[]{:S(2)}) async-start(bf16[4,256,512]{2,1,0:T(8,128)(2,1)} %fusion), calls=%async_computation.11 | async-start | bytes 2097152 | tf_op jit(solution)/shard_map/all_to_all | solution.py:70

commit v2 on v1

v2 whole, which is shorter than its diff:
```python
import jax
import jax.numpy as jnp
from jax import lax
from jax.experimental import pallas as pl
from jax.experimental.pallas import tpu as pltpu
from jax.sharding import Mesh
from jax.sharding import PartitionSpec as P

F32 = jnp.float32
BF16 = jnp.bfloat16
NARROW = ("x", "core")
NUM_Y, NUM_Z, NUM_X, NUM_CORE = 8, 8, 4, 2
NUM_NARROW = NUM_X * NUM_CORE


def spread(value, axis, count):
    copies = jnp.broadcast_to(value[None], (count,) + value.shape)
    return lax.all_to_all(copies, axis, 0, 0, tiled=True)


def total(stack):
    return stack.astype(F32).sum(0)


def product(factor, every):
    trail_rows, depth = factor.shape
    groups, steps, part, cols = every.shape
    rhs = groups * part
    own = trail_rows // NUM_NARROW

    def body(core_ref, factor_ref, every_ref, kept_ref, away_ref, flat_ref):
        @pl.when(pl.program_id(0) == 0)
        def _():
            for group in range(groups):
                for step in range(steps):
                    flat_ref[
                        group * part : (group + 1) * part,
                        step * cols : (step + 1) * cols,
                    ] = every_ref[group, step]

        core = core_ref[0]
        terms = (((1,), (1,)), ((), ()))
        kept_ref[0] = lax.dot_general(
            factor_ref[pl.ds(pl.multiple_of(core * own, own), own), :],
            flat_ref[...], terms, preferred_element_type=F32,
        )
        away_ref[0] = lax.dot_general(
            factor_ref[pl.ds(pl.multiple_of((1 - core) * own, own), own), :],
            flat_ref[...], terms, preferred_element_type=F32,
        ).astype(BF16)

    return pl.pallas_call(
        body,
        grid=(NUM_X,),
        in_specs=[
            pl.BlockSpec(memory_space=pltpu.SMEM),
            pl.BlockSpec((NUM_CORE * own, depth), lambda i: (i, 0)),
            pl.BlockSpec((groups, steps, part, cols), lambda i: (0, 0, 0, 0)),
        ],
        out_specs=[
            pl.BlockSpec((1, own, rhs), lambda i: (i, 0, 0)),
            pl.BlockSpec((1, own, rhs), lambda i: (i, 0, 0)),
        ],
        out_shape=[
            jax.ShapeDtypeStruct((NUM_X, own, rhs), F32),
            jax.ShapeDtypeStruct((NUM_X, own, rhs), BF16),
        ],
        scratch_shapes=[pltpu.VMEM((rhs, depth), BF16)],
        name="product",
    )(lax.axis_index("core").astype(jnp.int32)[None], factor, every)


def per_device(right_side, partial_in, window_factor, inverse_t, trailing_factor):
    steps, rows, rhs = right_side.shape
    cols = inverse_t.shape[2]
    part = rhs // NUM_Y
    slab = rows * NUM_Y
    trail_rows = trailing_factor.shape[0]

    first = (lax.axis_index(NARROW) == 0).astype(F32)
    terms = partial_in[0] - right_side.astype(F32) * first
    terms = terms.astype(BF16).reshape(steps, rows, NUM_Y, part).transpose(2, 0, 1, 3)
    terms = terms.reshape(NUM_Y, steps * rows * part // cols, cols)

    pairs = [(block, prior) for block in range(steps) for prior in range(block)]
    pieces = [window_factor[block, :, prior, :] for block, prior in pairs]
    pieces += [inverse_t[block] for block in range(steps)]
    pieces = jnp.concatenate(pieces)
    split = pieces.shape[0]
    copies = jnp.broadcast_to(pieces[None], (NUM_Y,) + pieces.shape)
    packed = lax.all_to_all(
        jnp.concatenate([copies, terms], axis=1), "y", 0, 0, tiled=True
    )
    terms = packed[:, split:].reshape(NUM_Y, steps, rows, part)
    terms = terms.transpose(1, 3, 0, 2).reshape(steps, part, slab).astype(F32)
    pieces = packed[:, :split].reshape(NUM_Y, -1, rows, cols)
    pieces = pieces.transpose(1, 0, 2, 3).reshape(-1, slab, cols)
    window = {pair: pieces[i] for i, pair in enumerate(pairs)}
    inverse = [pieces[len(pairs) + block] for block in range(steps)]

    solved_t = []
    for block in range(steps):
        fanned = terms[block]
        for prior in range(block):
            fanned = fanned + lax.dot_general(
                solved_t[prior], window[block, prior], (((1,), (1,)), ((), ())),
                preferred_element_type=F32,
            )
        fanned = total(spread(fanned.astype(BF16), NARROW, NUM_NARROW))
        residue = (-fanned).astype(BF16)
        share = jnp.dot(residue, inverse[block], preferred_element_type=F32)
        share = total(spread(share.astype(BF16), "z", NUM_Z))
        solved_t.append(share.astype(BF16))

    every = spread(jnp.stack(solved_t), "y", NUM_Y)
    solved = every.transpose(1, 3, 0, 2).reshape(steps, cols, rhs)

    flat_factor = trailing_factor.reshape(trail_rows, steps * cols)
    kept, away = product(flat_factor, every)
    back = lax.ppermute(away, "core", [(0, 1), (1, 0)])
    pair_sum = (kept + back.astype(F32)).astype(BF16)
    trailing = total(lax.all_to_all(pair_sum, "x", 0, 0, tiled=True))
    return (solved, trailing)


def solution(mesh):
    grid = Mesh(
        mesh.devices.reshape(NUM_Y, NUM_Z, NUM_X, NUM_CORE), ("y", "z", "x", "core")
    )
    wide = ("y", "z")
    placed = (
        P(None, wide, None),
        P(NARROW, None, wide, None),
        P(None, wide, None, NARROW),
        P(None, wide, NARROW),
        P(wide, None, NARROW),
    )
    return jax.shard_map(
        per_device,
        mesh=grid,
        in_specs=placed,
        out_specs=(P(None, NARROW, None), P(wide + NARROW, None)),
        check_vma=False,
    )
```

time: 233 us -> 180 us (0.77)
  local copies, waits for them, and re-layouts: 37.8 us -> 12.4 us
  waiting for transfers between devices: 83.8 us -> 62.9 us
  starting transfers between devices: 47.2 us -> 41.8 us
  Pallas kernels: 0 us -> 4.82 us
  matrix products: 4.61 us -> 1.32 us
  other arithmetic: 7.59 us -> 5.02 us
    all_to_all x0 -> x1, blocking collectives: none -> 20 us  [per_device(): lax.all_to_all(jnp.concatenate([copies, terms], axis=1), 'y', 0, 0, tiled...]
    all_to_all x4 -> x3, blocking collectives: 49.1 us -> 30 us  [spread(): return lax.all_to_all(copies, axis, 0, 0, tiled=True)]
    dynamic_slice x3 -> x0, local copies, waits for them, and re-layouts: 16.8 us -> none  [the longest x2 11.4 us: per_device(): kept = lax.dynamic_index_in_dim(trailing, core, 1, keepdims=False)]
    all_to_all x6, waiting for transfers between devices: 62.5 us -> 46.7 us  [spread(): return lax.all_to_all(copies, axis, 0, 0, tiled=True)]
    all_to_all x2 -> x1, starting transfers between devices: 11.9 us -> 3.65 us  [per_device(): trailing = total(lax.all_to_all(pair_sum, 'x', 0, 0, tiled=True))]
    all_to_all x2 -> x1, waiting for transfers between devices: 21.3 us -> 13.7 us  [per_device(): trailing = total(lax.all_to_all(pair_sum, 'x', 0, 0, tiled=True))]
    reshape x2 -> x3, local copies, waits for them, and re-layouts: 6.68 us -> 0.26 us  [the longest x2 0.15 us: per_device(): terms.astype(BF16).reshape(steps, rows, NUM_Y, part).transpose(2, 0, 1, 3)]
    pallas_call x0 -> x1, Pallas kernels: none -> 4.82 us  [product(): pl.pallas_call(body, grid=(NUM_X,), in_specs=[pl.BlockSpec(memory_space=p...]
  transfers between devices with their start and end apart: 9 -> 8, of which waited for: 8 -> 8; matrix products, arithmetic and copies ran while one was open for 6% -> 2% of each run, Pallas kernels for 0% -> 0%
where the time goes in v2:
time: 180 us; the launch traced here: 179 us
  waiting for transfers between devices  62.9 us (35%)
  blocking collectives  50 us (28%)
  starting transfers between devices  41.8 us (23%)
  local copies, waits for them, and re-layouts  12.4 us (7%)
  other arithmetic  5.02 us (3%)
  Pallas kernels  4.82 us (3%)
    all_to_all x6, waiting for transfers between devices, spread(): return lax.all_to_all(copies, axis, 0, 0, tiled=True)  46.7 us
    all_to_all x6, starting transfers between devices, spread(): return lax.all_to_all(copies, axis, 0, 0, tiled=True)  33.2 us
    all_to_all x3, blocking collectives, spread(): return lax.all_to_all(copies, axis, 0, 0, tiled=True)  30 us
    all_to_all x1, blocking collectives, per_device(): lax.all_to_all(jnp.concatenate([copies, terms], axis=1), 'y', 0, 0, tiled...  20 us
    all_to_all x1, waiting for transfers between devices, per_device(): trailing = total(lax.all_to_all(pair_sum, 'x', 0, 0, tiled=True))  13.7 us
    unnamed x17, local copies, waits for them, and re-layouts  5.6 us
    ppermute x1, starting transfers between devices, per_device(): back = lax.ppermute(away, 'core', [(0, 1), (1, 0)])  4.87 us
    pallas_call x1, Pallas kernels, product(): pl.pallas_call(body, grid=(NUM_X,), in_specs=[pl.BlockSpec(memory_space=p...  4.82 us
  transfers between devices with their start and end apart: 8, of which 8 were waited for; matrix products, arithmetic and copies ran while one was open for 2% of the time, Pallas kernels for 0%

profile of v2, /device:TPU:1, one launch (start us, length us, event | category | flops | bytes accessed | tf_op | source)
XLA Modules:
  0.0 179.1 jit_solution(1476383553934778020)
XLA Ops:
  5.7 20.0 %all_to_all.55 = bf16[8,192,128]{2,1,0:T(8,128)(2,1)S(1)} all-to-all(bf16[8,192,128]{2,1,0:T(8,128)(2,1)S(1)} %pad_maximum_fusion), channel_id=1, replica_groups=mesh['y'=8,'z'=8,'x'=4,'core'=2] {'y'}, dimensions={0} | all-to-all | bytes 786432 | tf_op jit(solution)/shard_map/all_to_all | solution.py:91
  26.6 7.4 %all-to-all-start.1 = ((bf16[8,64,128]{2,1,0:T(8,128)(2,1)}), bf16[8,64,128]{2,1,0:T(8,128)(2,1)S(1)}, u32[]{:S(2)}, u32[]{:S(2)}) async-start(bf16[8,64,128]{2,1,0:T(8,128)(2,1)} %broadcast_in_dim.26), calls=%async_computation.1 | async-start | bytes 262144 | tf_op jit(solution)/shard_map/all_to_all | solution.py:18
  34.0 5.2 %all-to-all-done.1 = bf16[8,64,128]{2,1,0:T(8,128)(2,1)S(1)} async-done(((bf16[8,64,128]{2,1,0:T(8,128)(2,1)}), bf16[8,64,128]{2,1,0:T(8,128)(2,1)S(1)}, u32[]{:S(2)}, u32[]{:S(2)}) %all-to-all-start.1) | async-done | bytes 131104 | tf_op jit(solution)/shard_map/all_to_all | solution.py:18
  40.1 10.0 %all-to-all-start.2 = ((bf16[8,64,128]{2,1,0:T(8,128)(2,1)}), bf16[8,64,128]{2,1,0:T(8,128)(2,1)S(1)}, u32[]{:S(2)}, u32[]{:S(2)}) async-start(bf16[8,64,128]{2,1,0:T(8,128)(2,1)} %broadcast_in_dim.27), calls=%async_computation.2 | async-start | bytes 262144 | tf_op jit(solution)/shard_map/all_to_all | solution.py:18
  50.2 7.8 %all-to-all-done.2 = bf16[8,64,128]{2,1,0:T(8,128)(2,1)S(1)} async-done(((bf16[8,64,128]{2,1,0:T(8,128)(2,1)}), bf16[8,64,128]{2,1,0:T(8,128)(2,1)S(1)}, u32[]{:S(2)}, u32[]{:S(2)}) %all-to-all-start.2) | async-done | bytes 131104 | tf_op jit(solution)/shard_map/all_to_all | solution.py:18
  58.1 10.0 %all_to_all.56 = bf16[8,64,128]{2,1,0:T(8,128)(2,1)S(1)} all-to-all(bf16[8,64,128]{2,1,0:T(8,128)(2,1)S(1)} %broadcast_in_dim.28), channel_id=1, replica_groups=mesh['y'=8,'z'=8,'x'=4,'core'=2] {'x','core'}, dimensions={0} | all-to-all | bytes 262144 | tf_op jit(solution)/shard_map/all_to_all | solution.py:18
  69.0 3.4 %all-to-all-start.4 = ((bf16[8,64,128]{2,1,0:T(8,128)(2,1)}), bf16[8,64,128]{2,1,0:T(8,128)(2,1)S(1)}, u32[]{:S(2)}, u32[]{:S(2)}) async-start(bf16[8,64,128]{2,1,0:T(8,128)(2,1)} %broadcast_in_dim.29), calls=%async_computation.4 | async-start | bytes 262144 | tf_op jit(solution)/shard_map/all_to_all | solution.py:18
  72.6 7.4 %all-to-all-done.4 = bf16[8,64,128]{2,1,0:T(8,128)(2,1)S(1)} async-done(((bf16[8,64,128]{2,1,0:T(8,128)(2,1)}), bf16[8,64,128]{2,1,0:T(8,128)(2,1)S(1)}, u32[]{:S(2)}, u32[]{:S(2)}) %all-to-all-start.4) | async-done | bytes 131104 | tf_op jit(solution)/shard_map/all_to_all | solution.py:18
  80.9 5.6 %all-to-all-start.5 = ((bf16[8,64,128]{2,1,0:T(8,128)(2,1)}), bf16[8,64,128]{2,1,0:T(8,128)(2,1)S(1)}, u32[]{:S(2)}, u32[]{:S(2)}) async-start(bf16[8,64,128]{2,1,0:T(8,128)(2,1)} %broadcast_in_dim.30), calls=%async_computation.5 | async-start | bytes 262144 | tf_op jit(solution)/shard_map/all_to_all | solution.py:18
  86.5 5.2 %all-to-all-done.5 = bf16[8,64,128]{2,1,0:T(8,128)(2,1)S(1)} async-done(((bf16[8,64,128]{2,1,0:T(8,128)(2,1)}), bf16[8,64,128]{2,1,0:T(8,128)(2,1)S(1)}, u32[]{:S(2)}, u32[]{:S(2)}) %all-to-all-start.5) | async-done | bytes 131104 | tf_op jit(solution)/shard_map/all_to_all | solution.py:18
  92.5 3.4 %all-to-all-start.6 = ((bf16[8,64,128]{2,1,0:T(8,128)(2,1)}), bf16[8,64,128]{2,1,0:T(8,128)(2,1)S(1)}, u32[]{:S(2)}, u32[]{:S(2)}) async-start(bf16[8,64,128]{2,1,0:T(8,128)(2,1)} %broadcast_in_dim.31), calls=%async_computation.6 | async-start | bytes 262144 | tf_op jit(solution)/shard_map/all_to_all | solution.py:18
  96.2 7.4 %all-to-all-done.6 = bf16[8,64,128]{2,1,0:T(8,128)(2,1)S(1)} async-done(((bf16[8,64,128]{2,1,0:T(8,128)(2,1)}), bf16[8,64,128]{2,1,0:T(8,128)(2,1)S(1)}, u32[]{:S(2)}, u32[]{:S(2)}) %all-to-all-start.6) | async-done | bytes 131104 | tf_op jit(solution)/shard_map/all_to_all | solution.py:18
  103.8 9.9 %all_to_all.57 = bf16[8,64,128]{2,1,0:T(8,128)(2,1)S(1)} all-to-all(bf16[8,64,128]{2,1,0:T(8,128)(2,1)S(1)} %broadcast_in_dim.32), channel_id=1, replica_groups=mesh['y'=8,'z'=8,'x'=4,'core'=2] {'x','core'}, dimensions={0} | all-to-all | bytes 262144 | tf_op jit(solution)/shard_map/all_to_all | solution.py:18
  113.9 10.1 %all_to_all.58 = bf16[8,64,128]{2,1,0:T(8,128)(2,1)S(1)} all-to-all(bf16[8,64,128]{2,1,0:T(8,128)(2,1)S(1)} %broadcast_in_dim.33), channel_id=1, replica_groups=mesh['y'=8,'z'=8,'x'=4,'core'=2] {'z'}, dimensions={0} | all-to-all | bytes 262144 | tf_op jit(solution)/shard_map/all_to_all | solution.py:18
  125.0 3.5 %all-to-all-start.9 = ((bf16[8,4,64,128]{3,2,1,0:T(8,128)(2,1)}), bf16[8,4,64,128]{3,2,1,0:T(8,128)(2,1)S(1)}, u32[]{:S(2)}, u32[]{:S(2)}) async-start(bf16[8,4,64,128]{3,2,1,0:T(8,128)(2,1)} %broadcast_in_dim.34), calls=%async_computation.9 | async-start | bytes 1048576 | tf_op jit(solution)/shard_map/all_to_all | solution.py:18
  128.5 1.7 copy.79
  130.1 13.7 %all-to-all-done.9.every_ref = bf16[8,4,64,128]{3,2,1,0:T(8,128)(2,1)S(1)} async-done(((bf16[8,4,64,128]{3,2,1,0:T(8,128)(2,1)}), bf16[8,4,64,128]{3,2,1,0:T(8,128)(2,1)S(1)}, u32[]{:S(2)}, u32[]{:S(2)}) %all-to-all-start.9) | async-done | bytes 524320 | tf_op jit(solution)/shard_map/all_to_all | solution.py:18
  144.7 4.8 %product.1 = (f32[4,256,512]{2,1,0:T(8,128)}, bf16[4,256,512]{2,1,0:T(8,128)(2,1)}) custom-call(s32[1]{0:T(128)} %bitcast.36.core_ref, bf16[2048,512]{1,0:T(8,128)(2,1)} %bitcast.87, bf16[8,4,64,128]{3,2,1,0:T(8,128)(2,1)} %copy-done), custom_call_target="tpu_custom_call" | custom-call | tf_op jit(solution)/shard_map/product/pallas_call | solution.py:52
  149.5 4.9 %collective-permute-start = (bf16[4,256,512]{2,1,0:T(8,128)(2,1)}, bf16[4,256,512]{2,1,0:T(8,128)(2,1)S(1)}, u32[]{:S(2)}, u32[]{:S(2)}) collective-permute-start(bf16[4,256,512]{2,1,0:T(8,128)(2,1)} %get-tuple-element.5), channel_id=1, source_target_pairs={{0,1},{1,0},{2,3},{3,2},{4,5},{5,4},{6,7},{7,6},{8,9},{9,8},{10,11... | collective-permute-start | bytes 3145736 | tf_op jit(solution)/shard_map/ppermute | solution.py:120
  154.3 2.5 %collective-permute-done = bf16[4,256,512]{2,1,0:T(8,128)(2,1)S(1)} collective-permute-done((bf16[4,256,512]{2,1,0:T(8,128)(2,1)}, bf16[4,256,512]{2,1,0:T(8,128)(2,1)S(1)}, u32[]{:S(2)}, u32[]{:S(2)}) %collective-permute-start) | collective-permute-done | bytes 1048608 | tf_op jit(solution)/shard_map/ppermute | solution.py:120
  156.8 2.9 %add_convert_fusion = bf16[4,256,512]{2,1,0:T(8,128)(2,1)} fusion(f32[4,256,512]{2,1,0:T(8,128)} %get-tuple-element.4, bf16[4,256,512]{2,1,0:T(8,128)(2,1)S(1)} %collective-permute-done), kind=kLoop, calls=%fused_computation.2 | loop fusion | flops 1572864 | bytes 4194304 | tf_op jit(solution)/shard_map/convert_element_type | solution.py:121
  159.7 3.6 %all-to-all-start.10 = ((bf16[4,256,512]{2,1,0:T(8,128)(2,1)}), bf16[4,256,512]{2,1,0:T(8,128)(2,1)S(1)}, u32[]{:S(2)}, u32[]{:S(2)}) async-start(bf16[4,256,512]{2,1,0:T(8,128)(2,1)} %add_convert_fusion), calls=%async_computation.10 | async-start | bytes 2097152 | tf_op jit(solution)/shard_map/all_to_all | solution.py:122
  163.5 1.0 copy.51
  164.5 13.7 %all-to-all-done.10 = bf16[4,256,512]{2,1,0:T(8,128)(2,1)S(1)} async-done(((bf16[4,256,512]{2,1,0:T(8,128)(2,1)}), bf16[4,256,512]{2,1,0:T(8,128)(2,1)S(1)}, u32[]{:S(2)}, u32[]{:S(2)}) %all-to-all-start.10) | async-done | bytes 1048608 | tf_op jit(solution)/shard_map/all_to_all | solution.py:122
  (64 shorter events, 13.2 us)
Async XLA Ops:
  26.6 12.6 %all-to-all-start.1 = ((bf16[8,64,128]{2,1,0:T(8,128)(2,1)}), bf16[8,64,128]{2,1,0:T(8,128)(2,1)S(1)}, u32[]{:S(2)}, u32[]{:S(2)}) async-start(bf16[8,64,128]{2,1,0:T(8,128)(2,1)} %broadcast_in_dim.26), calls=%async_computation.1 | async-start | bytes 262144 | tf_op jit(solution)/shard_map/all_to_all | solution.py:18
  40.1 17.9 %all-to-all-start.2 = ((bf16[8,64,128]{2,1,0:T(8,128)(2,1)}), bf16[8,64,128]{2,1,0:T(8,128)(2,1)S(1)}, u32[]{:S(2)}, u32[]{:S(2)}) async-start(bf16[8,64,128]{2,1,0:T(8,128)(2,1)} %broadcast_in_dim.27), calls=%async_computation.2 | async-start | bytes 262144 | tf_op jit(solution)/shard_map/all_to_all | solution.py:18
  69.0 11.0 %all-to-all-start.4 = ((bf16[8,64,128]{2,1,0:T(8,128)(2,1)}), bf16[8,64,128]{2,1,0:T(8,128)(2,1)S(1)}, u32[]{:S(2)}, u32[]{:S(2)}) async-start(bf16[8,64,128]{2,1,0:T(8,128)(2,1)} %broadcast_in_dim.29), calls=%async_computation.4 | async-start | bytes 262144 | tf_op jit(solution)/shard_map/all_to_all | solution.py:18
  80.9 10.8 %all-to-all-start.5 = ((bf16[8,64,128]{2,1,0:T(8,128)(2,1)}), bf16[8,64,128]{2,1,0:T(8,128)(2,1)S(1)}, u32[]{:S(2)}, u32[]{:S(2)}) async-start(bf16[8,64,128]{2,1,0:T(8,128)(2,1)} %broadcast_in_dim.30), calls=%async_computation.5 | async-start | bytes 262144 | tf_op jit(solution)/shard_map/all_to_all | solution.py:18
  86.4 42.0 %copy-start.2 = (bf16[2048,4,128]{2,1,0:T(4,128)(2,1)S(1)}, bf16[2048,4,128]{2,1,0:T(4,128)(2,1)}, u32[]{:S(2)}) copy-start(bf16[2048,4,128]{2,1,0:T(4,128)(2,1)} %param.9) | copy-start | bytes 6291460
  92.5 11.0 %all-to-all-start.6 = ((bf16[8,64,128]{2,1,0:T(8,128)(2,1)}), bf16[8,64,128]{2,1,0:T(8,128)(2,1)S(1)}, u32[]{:S(2)}, u32[]{:S(2)}) async-start(bf16[8,64,128]{2,1,0:T(8,128)(2,1)} %broadcast_in_dim.31), calls=%async_computation.6 | async-start | bytes 262144 | tf_op jit(solution)/shard_map/all_to_all | solution.py:18
  125.0 18.9 %all-to-all-start.9 = ((bf16[8,4,64,128]{3,2,1,0:T(8,128)(2,1)}), bf16[8,4,64,128]{3,2,1,0:T(8,128)(2,1)S(1)}, u32[]{:S(2)}, u32[]{:S(2)}) async-start(bf16[8,4,64,128]{3,2,1,0:T(8,128)(2,1)} %broadcast_in_dim.34), calls=%async_computation.9 | async-start | bytes 1048576 | tf_op jit(solution)/shard_map/all_to_all | solution.py:18
  143.9 0.8 copy-start
  149.5 7.4 %collective-permute-start = (bf16[4,256,512]{2,1,0:T(8,128)(2,1)}, bf16[4,256,512]{2,1,0:T(8,128)(2,1)S(1)}, u32[]{:S(2)}, u32[]{:S(2)}) collective-permute-start(bf16[4,256,512]{2,1,0:T(8,128)(2,1)} %get-tuple-element.5), channel_id=1, source_target_pairs={{0,1},{1,0},{2,3},{3,2},{4,5},{5,4},{6,7},{7,6},{8,9},{9,8},{10,11... | collective-permute-start | bytes 3145736 | tf_op jit(solution)/shard_map/ppermute | solution.py:120
  159.7 3.7 %copy-start.1 = (bf16[8,4,64,128]{3,2,1,0:T(8,128)(2,1)S(1)}, bf16[8,4,64,128]{3,2,1,0:T(8,128)(2,1)}, u32[]{:S(2)}) copy-start(bf16[8,4,64,128]{3,2,1,0:T(8,128)(2,1)} %copy-done) | copy-start | bytes 1572868
  159.7 18.4 %all-to-all-start.10 = ((bf16[4,256,512]{2,1,0:T(8,128)(2,1)}), bf16[4,256,512]{2,1,0:T(8,128)(2,1)S(1)}, u32[]{:S(2)}, u32[]{:S(2)}) async-start(bf16[4,256,512]{2,1,0:T(8,128)(2,1)} %add_convert_fusion), calls=%async_computation.10 | async-start | bytes 2097152 | tf_op jit(solution)/shard_map/all_to_all | solution.py:122

commit v3 on v1

v3 whole, which is shorter than its diff:
```python
import jax
import jax.numpy as jnp
from jax import lax
from jax.experimental import pallas as pl
from jax.experimental.pallas import tpu as pltpu
from jax.sharding import Mesh
from jax.sharding import PartitionSpec as P

F32 = jnp.float32
BF16 = jnp.bfloat16
NARROW = ("x", "core")
NUM_Y, NUM_Z, NUM_X, NUM_CORE = 8, 8, 4, 2
NUM_NARROW = NUM_X * NUM_CORE
SCRATCH = 8 * 2**20
ROWS_T = (((1,), (1,)), ((), ()))
VMEM = pl.BlockSpec(memory_space=pltpu.VMEM)
ANY = pl.BlockSpec(memory_space=pl.ANY)
SMEM = pl.BlockSpec(memory_space=pltpu.SMEM)


def resident(*arrays):
    return [pltpu.with_memory_space_constraint(array, pltpu.VMEM) for array in arrays]


def spread(value, axis, count):
    copies = jnp.broadcast_to(value[None], (count,) + value.shape)
    return lax.all_to_all(copies, axis, 0, 0, tiled=True)


def total(stack):
    return stack.astype(F32).sum(0)


def pairs_of(steps):
    return [(block, prior) for block in range(steps) for prior in range(block)]


def pack(right_side, partial_in, window_factor, inverse_t, first, ahead):
    steps, rows, rhs = right_side.shape
    cols = inverse_t.shape[2]
    part = rhs // NUM_Y
    pairs = pairs_of(steps)
    split = (len(pairs) + steps) * rows
    half = steps // 2

    def body(first_ref, right_ref, partial_ref, window_ref, inverse_ref, _, out_ref):
        for spot, (block, prior) in enumerate(pairs):
            piece = window_ref[block].astype(F32)[:, prior, :].astype(BF16)
            for y in range(NUM_Y):
                out_ref[y, spot * rows : (spot + 1) * rows, :] = piece
        for block in range(steps):
            spot = len(pairs) + block
            piece = inverse_ref[block]
            for y in range(NUM_Y):
                out_ref[y, spot * rows : (spot + 1) * rows, :] = piece
        taken = first_ref[0]
        for block in range(half):
            terms = [
                (partial_ref[0, k] - right_ref[k].astype(F32) * taken)
                for k in (block, block + half)
            ]
            spot = split + block * rows
            for y in range(NUM_Y):
                left, right = (t[:, y * part : (y + 1) * part] for t in terms)
                out_ref[y, spot : spot + rows, :] = jnp.concatenate(
                    [left, right], axis=1
                ).astype(BF16)

    return pl.pallas_call(
        body,
        in_specs=[SMEM, VMEM, VMEM, VMEM, VMEM, ANY],
        out_specs=VMEM,
        out_shape=pltpu.VMEM((NUM_Y, split + half * rows, cols), BF16),
        compiler_params=pltpu.CompilerParams(vmem_limit_bytes=SCRATCH),
        name="pack",
    )(first, right_side, partial_in, window_factor, inverse_t, ahead)


def unpack(packed, steps, rows, part):
    cols = packed.shape[2]
    slab = NUM_Y * rows
    pairs = pairs_of(steps)
    split = (len(pairs) + steps) * rows
    half = steps // 2

    def body(packed_ref, terms_ref, inverse_ref, *window_refs):
        for spot, (block, prior) in enumerate(pairs):
            for y in range(NUM_Y):
                window_refs[block - 1][
                    y * rows : (y + 1) * rows, prior * cols : (prior + 1) * cols
                ] = packed_ref[y, spot * rows : (spot + 1) * rows, :]
        for block in range(steps):
            spot = len(pairs) + block
            for y in range(NUM_Y):
                inverse_ref[block, y * rows : (y + 1) * rows, :] = packed_ref[
                    y, spot * rows : (spot + 1) * rows, :
                ]
        for block in range(half):
            spot = split + block * rows
            stack = jnp.concatenate(
                [packed_ref[y, spot : spot + rows, :] for y in range(NUM_Y)], axis=0
            )
            turned = stack.astype(F32).T
            terms_ref[block] = turned[:part]
            terms_ref[block + half] = turned[part:]

    outs = [
        pltpu.VMEM((steps, part, slab), F32),
        pltpu.VMEM((steps, slab, cols), BF16),
    ] + [pltpu.VMEM((slab, cols * k), BF16) for k in range(1, steps)]
    return pl.pallas_call(
        body,
        in_specs=[VMEM],
        out_specs=[VMEM] * len(outs),
        out_shape=outs,
        compiler_params=pltpu.CompilerParams(vmem_limit_bytes=SCRATCH),
        name="unpack",
    )(*resident(packed))


def turn(every):
    groups, steps, part, cols = every.shape

    def body(every_ref, out_ref):
        for step in range(steps):
            stack = jnp.concatenate(
                [every_ref[group, step] for group in range(groups)], axis=0
            )
            out_ref[step] = stack.T

    return pl.pallas_call(
        body,
        in_specs=[VMEM],
        out_specs=VMEM,
        out_shape=pltpu.HBM((steps, cols, groups * part), BF16),
        compiler_params=pltpu.CompilerParams(vmem_limit_bytes=SCRATCH),
        name="turn",
    )(*resident(every))


def product(core, factor, every, back=None):
    trail_rows, depth = factor.shape
    groups, steps, part, cols = every.shape
    rhs = groups * part
    own = trail_rows // NUM_NARROW

    def body(core_ref, factor_ref, every_ref, *refs):
        out_ref, flat_ref = refs[-2:]
        side = 1 - core_ref[0] if back is None else core_ref[0]
        for group in range(groups):
            for step in range(steps):
                flat_ref[
                    group * part : (group + 1) * part,
                    step * cols : (step + 1) * cols,
                ] = every_ref[group, step]

        @pl.loop(0, NUM_X)
        def _(i):
            row = pl.multiple_of((NUM_CORE * i + side) * own, own)
            value = lax.dot_general(
                factor_ref[pl.ds(row, own), :], flat_ref[...], ROWS_T,
                preferred_element_type=F32,
            )
            if back is not None:
                value = value + refs[0][i].astype(F32)
            out_ref[i] = value.astype(BF16)

    arrays = resident(factor, every) + ([] if back is None else resident(back[0]))
    after = []
    if back is not None:
        after = [pltpu.with_memory_space_constraint(back[1], pltpu.HBM)]
    return pl.pallas_call(
        body,
        in_specs=[SMEM] + [VMEM] * len(arrays) + [ANY] * len(after),
        out_specs=VMEM,
        scratch_shapes=[pltpu.VMEM((rhs, depth), BF16)],
        out_shape=pltpu.VMEM((NUM_X, own, rhs), BF16),
        compiler_params=pltpu.CompilerParams(vmem_limit_bytes=SCRATCH),
        name="product",
    )(core, *arrays, *after)


def per_device(right_side, partial_in, window_factor, inverse_t, trailing_factor):
    steps, rows, rhs = right_side.shape
    cols = inverse_t.shape[2]
    part = rhs // NUM_Y
    trail_rows = trailing_factor.shape[0]

    first = (lax.axis_index(NARROW) == 0).astype(F32)[None]
    flat_factor = trailing_factor.reshape(trail_rows, steps * cols)
    packed = pack(right_side, partial_in, window_factor, inverse_t, first, flat_factor)
    packed = lax.all_to_all(packed, "y", 0, 0, tiled=True)
    terms, inverse, *window = unpack(packed, steps, rows, part)

    solved_t = []
    for block in range(steps):
        fanned = terms[block]
        if block:
            fanned = fanned + lax.dot_general(
                jnp.concatenate(solved_t, axis=1), window[block - 1], ROWS_T,
                preferred_element_type=F32,
            )
        fanned = total(spread(fanned.astype(BF16), NARROW, NUM_NARROW))
        residue = (-fanned).astype(BF16)
        share = jnp.dot(residue, inverse[block], preferred_element_type=F32)
        share = total(spread(share.astype(BF16), "z", NUM_Z))
        solved_t.append(share.astype(BF16))

    every = spread(jnp.stack(solved_t), "y", NUM_Y)

    core = lax.axis_index("core").astype(jnp.int32)[None]
    away = product(core, flat_factor, every)
    back = lax.ppermute(away, "core", [(0, 1), (1, 0)])
    solved = turn(every)
    kept = product(core, flat_factor, every, (back, solved))
    trailing = total(lax.all_to_all(kept, "x", 0, 0, tiled=True))
    return (solved, trailing)


def solution(mesh):
    grid = Mesh(
        mesh.devices.reshape(NUM_Y, NUM_Z, NUM_X, NUM_CORE), ("y", "z", "x", "core")
    )
    wide = ("y", "z")
    placed = (
        P(None, wide, None),
        P(NARROW, None, wide, None),
        P(None, wide, None, NARROW),
        P(None, wide, NARROW),
        P(wide, None, NARROW),
    )
    return jax.shard_map(
        per_device,
        mesh=grid,
        in_specs=placed,
        out_specs=(P(None, NARROW, None), P(wide + NARROW, None)),
        check_vma=False,
    )
```

time: 233 us -> 161 us (0.69)
  blocking collectives: 49.1 us -> 145 us
  waiting for transfers between devices: 83.8 us -> 1.28 us
  starting transfers between devices: 47.2 us -> 5.74 us
  local copies, waits for them, and re-layouts: 37.8 us -> 2.37 us
  other arithmetic: 7.59 us -> 1.13 us
  Pallas kernels: 0 us -> 4.03 us
  matrix products: 4.61 us -> 0.93 us
    all_to_all x8 -> x0, waiting for transfers between devices: 83.8 us -> none  [the longest x6 62.5 us: spread(): return lax.all_to_all(copies, axis, 0, 0, tiled=True)]
    all_to_all x4 -> x9, blocking collectives: 49.1 us -> 107 us  [spread(): return lax.all_to_all(copies, axis, 0, 0, tiled=True)]
    all_to_all x8 -> x0, starting transfers between devices: 41.9 us -> none  [the longest x6 30.1 us: spread(): return lax.all_to_all(copies, axis, 0, 0, tiled=True)]
    all_to_all x0 -> x2, blocking collectives: none -> 37.2 us  [the longest x1 20 us: per_device(): packed = lax.all_to_all(packed, 'y', 0, 0, tiled=True)]
    dynamic_slice x3 -> x0, local copies, waits for them, and re-layouts: 16.8 us -> none  [the longest x2 11.4 us: per_device(): kept = lax.dynamic_index_in_dim(trailing, core, 1, keepdims=False)]
    reshape x2 -> x0, local copies, waits for them, and re-layouts: 6.68 us -> none  [the longest x1 6.58 us: per_device(): trailing = trailing.reshape(NUM_X, NUM_CORE, own, rhs)]
    unnamed x14 -> x9, local copies, waits for them, and re-layouts: 7.83 us -> 2.03 us
    broadcast_in_dim x11 -> x10, local copies, waits for them, and re-layouts: 4.82 us -> 0.34 us  [spread(): copies = jnp.broadcast_to(value[None], (count,) + value.shape)]
  transfers between devices with their start and end apart: 9 -> 1, of which waited for: 8 -> 1; matrix products, arithmetic and copies ran while one was open for 6% -> 0% of each run, Pallas kernels for 0% -> 1%
where the time goes in v3:
time: 161 us
  blocking collectives  145 us (90%)
  starting transfers between devices  5.74 us (4%)
  Pallas kernels  4.03 us (3%)
  local copies, waits for them, and re-layouts  2.37 us (1%)
    all_to_all x9, blocking collectives, spread(): return lax.all_to_all(copies, axis, 0, 0, tiled=True)  107 us
    all_to_all x1, blocking collectives, per_device(): packed = lax.all_to_all(packed, 'y', 0, 0, tiled=True)  20 us
    all_to_all x1, blocking collectives, per_device(): trailing = total(lax.all_to_all(kept, 'x', 0, 0, tiled=True))  17.2 us
    ppermute x1, starting transfers between devices, per_device(): back = lax.ppermute(away, 'core', [(0, 1), (1, 0)])  5.74 us
  transfers between devices with their start and end apart: 1, of which 1 were waited for; matrix products, arithmetic and copies ran while one was open for 0% of the time, Pallas kernels for 1%

profile of v3, /device:TPU:1, one launch (start us, length us, event | category | flops | bytes accessed | tf_op | source)
XLA Modules:
  0.0 160.9 jit_solution(13782988632675813378)
XLA Ops:
  0.7 2.0 %copy.9 = bf16[256,8,4,128]{3,1,2,0:T(8,128)(2,1)S(1)} copy(bf16[256,8,4,128]{3,2,1,0:T(4,128)(2,1)} %bitcast.37) | data formatting | bytes 4194304
  2.8 20.0 %all_to_all.55.packed_ref = bf16[8,192,128]{2,1,0:T(8,128)(2,1)S(1)} all-to-all(bf16[8,192,128]{2,1,0:T(8,128)(2,1)S(1)} %pack.1), channel_id=1, replica_groups=mesh['y'=8,'z'=8,'x'=4,'core'=2] {'y'}, dimensions={0} | all-to-all | bytes 786432 | tf_op jit(solution)/shard_map/all_to_all | solution.py:192
  22.9 12.4 %all_to_all.56 = bf16[8,64,128]{2,1,0:T(8,128)(2,1)S(1)} all-to-all(bf16[8,64,128]{2,1,0:T(8,128)(2,1)S(1)} %broadcast_in_dim.29), channel_id=1, replica_groups=mesh['y'=8,'z'=8,'x'=4,'core'=2] {'x','core'}, dimensions={0} | all-to-all | bytes 262144 | tf_op jit(solution)/shard_map/all_to_all | solution.py:27
  35.4 0.1 convolution_convert_fusion.3
  35.6 17.7 %all_to_all.57 = bf16[8,64,128]{2,1,0:T(8,128)(2,1)S(1)} all-to-all(bf16[8,64,128]{2,1,0:T(8,128)(2,1)S(1)} %broadcast_in_dim.30), channel_id=1, replica_groups=mesh['y'=8,'z'=8,'x'=4,'core'=2] {'z'}, dimensions={0} | all-to-all | bytes 262144 | tf_op jit(solution)/shard_map/all_to_all | solution.py:27
  53.3 0.1 fusion
  53.5 10.0 %all_to_all.58 = bf16[8,64,128]{2,1,0:T(8,128)(2,1)S(1)} all-to-all(bf16[8,64,128]{2,1,0:T(8,128)(2,1)S(1)} %broadcast_in_dim.31), channel_id=1, replica_groups=mesh['y'=8,'z'=8,'x'=4,'core'=2] {'x','core'}, dimensions={0} | all-to-all | bytes 262144 | tf_op jit(solution)/shard_map/all_to_all | solution.py:27
  63.5 0.1 convolution_convert_fusion.2
  63.7 10.1 %all_to_all.59 = bf16[8,64,128]{2,1,0:T(8,128)(2,1)S(1)} all-to-all(bf16[8,64,128]{2,1,0:T(8,128)(2,1)S(1)} %broadcast_in_dim.32), channel_id=1, replica_groups=mesh['y'=8,'z'=8,'x'=4,'core'=2] {'z'}, dimensions={0} | all-to-all | bytes 262144 | tf_op jit(solution)/shard_map/all_to_all | solution.py:27
  73.8 0.1 fusion.1
  74.0 9.9 %all_to_all.60 = bf16[8,64,128]{2,1,0:T(8,128)(2,1)S(1)} all-to-all(bf16[8,64,128]{2,1,0:T(8,128)(2,1)S(1)} %broadcast_in_dim.33), channel_id=1, replica_groups=mesh['y'=8,'z'=8,'x'=4,'core'=2] {'x','core'}, dimensions={0} | all-to-all | bytes 262144 | tf_op jit(solution)/shard_map/all_to_all | solution.py:27
  83.9 0.1 convolution_convert_fusion.1
  84.1 10.1 %all_to_all.61 = bf16[8,64,128]{2,1,0:T(8,128)(2,1)S(1)} all-to-all(bf16[8,64,128]{2,1,0:T(8,128)(2,1)S(1)} %broadcast_in_dim.34), channel_id=1, replica_groups=mesh['y'=8,'z'=8,'x'=4,'core'=2] {'z'}, dimensions={0} | all-to-all | bytes 262144 | tf_op jit(solution)/shard_map/all_to_all | solution.py:27
  94.2 0.2 fusion.2
  94.4 9.9 %all_to_all.62 = bf16[8,64,128]{2,1,0:T(8,128)(2,1)S(1)} all-to-all(bf16[8,64,128]{2,1,0:T(8,128)(2,1)S(1)} %broadcast_in_dim.35), channel_id=1, replica_groups=mesh['y'=8,'z'=8,'x'=4,'core'=2] {'x','core'}, dimensions={0} | all-to-all | bytes 262144 | tf_op jit(solution)/shard_map/all_to_all | solution.py:27
  104.5 10.1 %all_to_all.63 = bf16[8,64,128]{2,1,0:T(8,128)(2,1)S(1)} all-to-all(bf16[8,64,128]{2,1,0:T(8,128)(2,1)S(1)} %broadcast_in_dim.36), channel_id=1, replica_groups=mesh['y'=8,'z'=8,'x'=4,'core'=2] {'z'}, dimensions={0} | all-to-all | bytes 262144 | tf_op jit(solution)/shard_map/all_to_all | solution.py:27
  114.8 17.0 %all_to_all.64.every_ref = bf16[8,4,64,128]{3,2,1,0:T(8,128)(2,1)S(1)} all-to-all(bf16[8,4,64,128]{3,2,1,0:T(8,128)(2,1)S(1)} %broadcast_in_dim.37), channel_id=1, replica_groups=mesh['y'=8,'z'=8,'x'=4,'core'=2] {'y'}, dimensions={0} | all-to-all | bytes 1048576 | tf_op jit(solution)/shard_map/all_to_all | solution.py:27
  131.8 1.4 product.2
  133.3 5.7 %collective-permute-start = (bf16[4,256,512]{2,1,0:T(8,128)(2,1)S(1)}, bf16[4,256,512]{2,1,0:T(8,128)(2,1)S(1)}, u32[]{:S(2)}, u32[]{:S(2)}) collective-permute-start(bf16[4,256,512]{2,1,0:T(8,128)(2,1)S(1)} %product.2), channel_id=1, source_target_pairs={{0,1},{1,0},{2,3},{3,2},{4,5},{5,4},{6,7},{7,6},{8,9},{9,8},{10,11... | collective-permute-start | bytes 3145736 | tf_op jit(solution)/shard_map/ppermute | solution.py:213
  139.0 1.0 turn.1.refs_1_
  140.0 1.3 collective-permute-done.refs_0_
  141.3 1.4 product.3
  142.7 17.2 %all_to_all.65 = bf16[4,256,512]{2,1,0:T(8,128)(2,1)S(1)} all-to-all(bf16[4,256,512]{2,1,0:T(8,128)(2,1)S(1)} %product.3), channel_id=1, replica_groups=mesh['y'=8,'z'=8,'x'=4,'core'=2] {'x'}, dimensions={0} | all-to-all | bytes 2097152 | tf_op jit(solution)/shard_map/all_to_all | solution.py:216
  159.9 0.9 convert_reduce_fusion
  (30 shorter events, 0.9 us)
Async XLA Ops:
  0.6 2.1 %copy-start = (f32[1,4,16,512]{3,2,1,0:T(8,128)S(1)}, f32[1,4,16,512]{3,2,1,0:T(8,128)}, u32[]{:S(2)}) copy-start(f32[1,4,16,512]{3,2,1,0:T(8,128)} %partial_ref.1) | copy-start | bytes 393220
  0.7 2.1 %copy-start.1 = (bf16[4,16,512]{2,1,0:T(8,128)(2,1)S(1)}, bf16[4,16,512]{2,1,0:T(8,128)(2,1)}, u32[]{:S(2)}) copy-start(bf16[4,16,512]{2,1,0:T(8,128)(2,1)} %right_ref.1) | copy-start | bytes 196612
  0.7 2.1 %copy-start.2 = (bf16[4,16,4,128]{3,2,1,0:T(4,128)(2,1)S(1)}, bf16[4,16,4,128]{3,2,1,0:T(4,128)(2,1)}, u32[]{:S(2)}) copy-start(bf16[4,16,4,128]{3,2,1,0:T(4,128)(2,1)} %window_ref.1) | copy-start | bytes 196612
  0.7 2.1 %copy-start.3 = (bf16[4,16,128]{2,1,0:T(8,128)(2,1)S(1)}, bf16[4,16,128]{2,1,0:T(8,128)(2,1)}, u32[]{:S(2)}) copy-start(bf16[4,16,128]{2,1,0:T(8,128)(2,1)} %inverse_ref.1) | copy-start | bytes 49156
  133.3 8.0 %collective-permute-start = (bf16[4,256,512]{2,1,0:T(8,128)(2,1)S(1)}, bf16[4,256,512]{2,1,0:T(8,128)(2,1)S(1)}, u32[]{:S(2)}, u32[]{:S(2)}) collective-permute-start(bf16[4,256,512]{2,1,0:T(8,128)(2,1)S(1)} %product.2), channel_id=1, source_target_pairs={{0,1},{1,0},{2,3},{3,2},{4,5},{5,4},{6,7},{7,6},{8,9},{9,8},{10,11... | collective-permute-start | bytes 3145736 | tf_op jit(solution)/shard_map/ppermute | solution.py:213

commit v4 on v3

--- a/solution.py
+++ b/solution.py
@@ -11,6 +11,7 @@
 NARROW = ("x", "core")
 NUM_Y, NUM_Z, NUM_X, NUM_CORE = 8, 8, 4, 2
 NUM_NARROW = NUM_X * NUM_CORE
+STEPS = 4
 SCRATCH = 8 * 2**20
 ROWS_T = (((1,), (1,)), ((), ()))
 VMEM = pl.BlockSpec(memory_space=pltpu.VMEM)
@@ -76,83 +77,163 @@
     )(first, right_side, partial_in, window_factor, inverse_t, ahead)
 
 
-def unpack(packed, steps, rows, part):
+def unpack(packed, native, rows, part):
     cols = packed.shape[2]
     slab = NUM_Y * rows
-    pairs = pairs_of(steps)
-    split = (len(pairs) + steps) * rows
-    half = steps // 2
-
-    def body(packed_ref, terms_ref, inverse_ref, *window_refs):
-        for spot, (block, prior) in enumerate(pairs):
-            for y in range(NUM_Y):
-                window_refs[block - 1][
-                    y * rows : (y + 1) * rows, prior * cols : (prior + 1) * cols
-                ] = packed_ref[y, spot * rows : (spot + 1) * rows, :]
-        for block in range(steps):
+    pairs = pairs_of(STEPS)
+    split = (len(pairs) + STEPS) * rows
+
+    def body(
+        packed_ref, native_ref, early_ref, late_ref, inverse_ref,
+        one_ref, two_ref, last_ref, own_ref,
+    ):
+        own_ref[...] = native_ref[2]
+        target = {
+            (1, 0): (one_ref, 0, 0),
+            (2, 0): (two_ref, 0, 0),
+            (2, 1): (two_ref, 0, cols),
+            (3, 0): (two_ref, slab, 0),
+            (3, 1): (two_ref, slab, cols),
+            (3, 2): (last_ref, 0, 0),
+        }
+        for spot, pair in enumerate(pairs):
+            ref, row, col = target[pair]
+            for y in range(NUM_Y):
+                ref[row + y * rows : row + (y + 1) * rows, col : col + cols] = (
+                    packed_ref[y, spot * rows : (spot + 1) * rows, :]
+                )
+        for block in range(STEPS):
             spot = len(pairs) + block
             for y in range(NUM_Y):
                 inverse_ref[block, y * rows : (y + 1) * rows, :] = packed_ref[
                     y, spot * rows : (spot + 1) * rows, :
                 ]
-        for block in range(half):
+        for block in range(2):
             spot = split + block * rows
             stack = jnp.concatenate(
                 [packed_ref[y, spot : spot + rows, :] for y in range(NUM_Y)], axis=0
             )
             turned = stack.astype(F32).T
-            terms_ref[block] = turned[:part]
-            terms_ref[block + half] = turned[part:]
+            early_ref[block] = turned[:part]
+            late_ref[:, block * slab : (block + 1) * slab] = turned[part:]
 
     outs = [
-        pltpu.VMEM((steps, part, slab), F32),
-        pltpu.VMEM((steps, slab, cols), BF16),
-    ] + [pltpu.VMEM((slab, cols * k), BF16) for k in range(1, steps)]
-    return pl.pallas_call(
-        body,
-        in_specs=[VMEM],
+        pltpu.VMEM((2, part, slab), F32),
+        pltpu.VMEM((part, 2 * slab), F32),
+        pltpu.VMEM((STEPS, slab, cols), BF16),
+        pltpu.VMEM((slab, cols), BF16),
+        pltpu.VMEM((2 * slab, 2 * cols), BF16),
+        pltpu.VMEM((slab, cols), BF16),
+        pltpu.VMEM((rows, cols), BF16),
+    ]
+    return pl.pallas_call(
+        body,
+        in_specs=[VMEM, VMEM],
         out_specs=[VMEM] * len(outs),
         out_shape=outs,
         compiler_params=pltpu.CompilerParams(vmem_limit_bytes=SCRATCH),
         name="unpack",
-    )(*resident(packed))
-
-
-def turn(every):
-    groups, steps, part, cols = every.shape
-
-    def body(every_ref, out_ref):
-        for step in range(steps):
-            stack = jnp.concatenate(
-                [every_ref[group, step] for group in range(groups)], axis=0
+    )(*resident(packed, native))
+
+
+def fan(terms, solved, window, ahead):
+    part, cols = terms.shape[0], solved.shape[1]
+
+    def body(terms_ref, solved_ref, window_ref, _, out_ref):
+        value = terms_ref[...]
+        for block in range(2):
+            value = value + lax.dot_general(
+                solved_ref[block * part : (block + 1) * part, :],
+                window_ref[:, block * cols : (block + 1) * cols],
+                ROWS_T, preferred_element_type=F32,
             )
-            out_ref[step] = stack.T
-
-    return pl.pallas_call(
-        body,
-        in_specs=[VMEM],
-        out_specs=VMEM,
-        out_shape=pltpu.HBM((steps, cols, groups * part), BF16),
+        value = value.astype(BF16)
+        for n in range(NUM_NARROW):
+            out_ref[n] = value
+
+    return pl.pallas_call(
+        body,
+        in_specs=[VMEM] * 3 + [ANY],
+        out_specs=VMEM,
+        out_shape=pltpu.VMEM((NUM_NARROW,) + terms.shape, BF16),
+        compiler_params=pltpu.CompilerParams(vmem_limit_bytes=SCRATCH),
+        name="fan",
+    )(*resident(terms, solved, window), ahead)
+
+
+def pair(fanned, inverse, early):
+    part, wide_cols = fanned.shape[1:]
+    slab, cols = inverse.shape[1:]
+    rows = slab // NUM_Y
+
+    def body(fanned_ref, inverse_ref, early_ref, out_ref):
+        residue = fanned_ref[0].astype(F32)
+        for n in range(1, NUM_NARROW):
+            residue = residue + fanned_ref[n].astype(F32)
+        residue = (-residue).astype(BF16)
+        two, three = residue[:, :slab], residue[:, slab:]
+        link = jnp.concatenate(
+            [early_ref[y, 2 * part : 2 * part + rows, :] for y in range(NUM_Y)], axis=0
+        )
+        left = jnp.dot(two, inverse_ref[2], preferred_element_type=F32)
+        right = jnp.dot(three, inverse_ref[3], preferred_element_type=F32)
+        right = right + jnp.dot(two, link, preferred_element_type=F32)
+        for z in range(NUM_Z):
+            out_ref[z, :, :cols] = left.astype(BF16)
+            out_ref[z, :, cols:] = right.astype(BF16)
+
+    return pl.pallas_call(
+        body,
+        in_specs=[VMEM] * 3,
+        out_specs=VMEM,
+        out_shape=pltpu.VMEM((NUM_Z, part, 2 * cols), BF16),
+        compiler_params=pltpu.CompilerParams(vmem_limit_bytes=SCRATCH),
+        name="pair",
+    )(*resident(fanned, inverse, early))
+
+
+def flatten(early_ref, late_ref, flat_ref):
+    part, late_cols = late_ref.shape[1:]
+    cols = late_cols // 2
+    for y in range(NUM_Y):
+        span = slice(y * part, (y + 1) * part)
+        for block in range(2):
+            flat_ref[span, block * cols : (block + 1) * cols] = early_ref[
+                y, block * part : (block + 1) * part, :
+            ]
+        flat_ref[span, 2 * cols :] = late_ref[y]
+
+
+def turn(early, late):
+    part, late_cols = late.shape[1:]
+    rhs = NUM_Y * part
+    cols = late_cols // 2
+
+    def body(early_ref, late_ref, out_ref, flat_ref):
+        flatten(early_ref, late_ref, flat_ref)
+        for step in range(STEPS):
+            out_ref[step] = flat_ref[:, step * cols : (step + 1) * cols].T
+
+    return pl.pallas_call(
+        body,
+        in_specs=[VMEM, VMEM],
+        out_specs=VMEM,
+        scratch_shapes=[pltpu.VMEM((rhs, STEPS * cols), BF16)],
+        out_shape=pltpu.HBM((STEPS, cols, rhs), BF16),
         compiler_params=pltpu.CompilerParams(vmem_limit_bytes=SCRATCH),
         name="turn",
-    )(*resident(every))
-
-
-def product(core, factor, every, back=None):
+    )(*resident(early, late))
+
+
+def product(core, factor, early, late, back=None):
     trail_rows, depth = factor.shape
-    groups, steps, part, cols = every.shape
-    rhs = groups * part
+    rhs = NUM_Y * late.shape[1]
     own = trail_rows // NUM_NARROW
 
-    def body(core_ref, factor_ref, every_ref, *refs):
+    def body(core_ref, factor_ref, early_ref, late_ref, *refs):
         out_ref, flat_ref = refs[-2:]
         side = 1 - core_ref[0] if back is None else core_ref[0]
-        for group in range(groups):
-            for step in range(steps):
-                flat_ref[
-                    group * part : (group + 1) * part,
-                    step * cols : (step + 1) * cols,
-                ] = every_ref[group, step]
+        flatten(early_ref, late_ref, flat_ref)
 
         @pl.loop(0, NUM_X)
         def _(i):
@@ -165,7 +246,7 @@
                 value = value + refs[0][i].astype(F32)
             out_ref[i] = value.astype(BF16)
 
-    arrays = resident(factor, every) + ([] if back is None else resident(back[0]))
+    arrays = resident(factor, early, late) + ([] if back is None else resident(back[0]))
     after = []
     if back is not None:
         after = [pltpu.with_memory_space_constraint(back[1], pltpu.HBM)]
@@ -190,29 +271,49 @@
     flat_factor = trailing_factor.reshape(trail_rows, steps * cols)
     packed = pack(right_side, partial_in, window_factor, inverse_t, first, flat_factor)
     packed = lax.all_to_all(packed, "y", 0, 0, tiled=True)
-    terms, inverse, *window = unpack(packed, steps, rows, part)
-
-    solved_t = []
-    for block in range(steps):
-        fanned = terms[block]
-        if block:
-            fanned = fanned + lax.dot_general(
-                jnp.concatenate(solved_t, axis=1), window[block - 1], ROWS_T,
-                preferred_element_type=F32,
-            )
-        fanned = total(spread(fanned.astype(BF16), NARROW, NUM_NARROW))
-        residue = (-fanned).astype(BF16)
-        share = jnp.dot(residue, inverse[block], preferred_element_type=F32)
-        share = total(spread(share.astype(BF16), "z", NUM_Z))
-        solved_t.append(share.astype(BF16))
-
-    every = spread(jnp.stack(solved_t), "y", NUM_Y)
+    first_terms, late_terms, inverse, window_one, window_two, window_last, own = unpack(
+        packed, inverse_t, rows, part
+    )
+
+    def over_narrow(value):
+        return total(spread(value.astype(BF16), NARROW, NUM_NARROW))
+
+    residue = (-over_narrow(first_terms[0])).astype(BF16)
+    share = jnp.dot(residue, inverse[0], preferred_element_type=F32).astype(BF16)
+    got = spread(jnp.concatenate([share, own]), "z", NUM_Z)
+    solved_0 = total(got[:, :part]).astype(BF16)
+    ahead = got[:, part:].reshape(NUM_Z * rows, cols)
+
+    fanned = first_terms[1] + lax.dot_general(
+        solved_0, window_one, ROWS_T, preferred_element_type=F32
+    )
+    link = lax.dot_general(window_last, ahead, ROWS_T, preferred_element_type=F32)
+    both = over_narrow(jnp.concatenate([fanned, link]))
+    residue, link = (-both[:part]).astype(BF16), (-both[part:]).astype(BF16)
+    share = jnp.dot(residue, inverse[1], preferred_element_type=F32).astype(BF16)
+    link = lax.dot_general(
+        link, inverse[3], (((0,), (0,)), ((), ())), preferred_element_type=F32
+    )
+    copies = jnp.broadcast_to(share[None], (NUM_Z,) + share.shape)
+    link = link.astype(BF16).reshape(NUM_Z, rows, cols)
+    got = lax.all_to_all(
+        jnp.concatenate([copies, link], axis=1), "z", 0, 0, tiled=True
+    )
+    got = total(got).astype(BF16)
+
+    stack = jnp.concatenate([solved_0, got])
+    early = spread(stack, "y", NUM_Y)
+    fanned = fan(late_terms, stack, window_two, early)
+    fanned = lax.all_to_all(fanned, NARROW, 0, 0, tiled=True)
+    share = pair(fanned, inverse, early)
+    late = total(lax.all_to_all(share, "z", 0, 0, tiled=True)).astype(BF16)
+    late = spread(late, "y", NUM_Y)
 
     core = lax.axis_index("core").astype(jnp.int32)[None]
-    away = product(core, flat_factor, every)
+    away = product(core, flat_factor, early, late)
     back = lax.ppermute(away, "core", [(0, 1), (1, 0)])
-    solved = turn(every)
-    kept = product(core, flat_factor, every, (back, solved))
+    solved = turn(early, late)
+    kept = product(core, flat_factor, early, late, (back, solved))
     trailing = total(lax.all_to_all(kept, "x", 0, 0, tiled=True))
     return (solved, trailing)
 

time: 161 us -> 157 us (0.975)
  blocking collectives: 145 us -> 141 us
    all_to_all x9 -> x5, blocking collectives: 107 us -> 67.5 us  [spread(): return lax.all_to_all(copies, axis, 0, 0, tiled=True)]
    all_to_all x0 -> x3, blocking collectives: none -> 35.9 us  [the longest x1 12.6 us: per_device(): late = total(lax.all_to_all(share, 'z', 0, 0, tiled=True)).astype(BF16)]
where the time goes in v4:
time: 157 us
  blocking collectives  141 us (90%)
  starting transfers between devices  5.61 us (4%)
  Pallas kernels  4.33 us (3%)
  local copies, waits for them, and re-layouts  2.22 us (1%)
    all_to_all x5, blocking collectives, spread(): return lax.all_to_all(copies, axis, 0, 0, tiled=True)  67.5 us
    all_to_all x1, blocking collectives, per_device(): packed = lax.all_to_all(packed, 'y', 0, 0, tiled=True)  20 us
    all_to_all x1, blocking collectives, per_device(): trailing = total(lax.all_to_all(kept, 'x', 0, 0, tiled=True))  17.2 us
    all_to_all x1, blocking collectives, per_device(): late = total(lax.all_to_all(share, 'z', 0, 0, tiled=True)).astype(BF16)  12.6 us
    all_to_all x1, blocking collectives, per_device(): fanned = lax.all_to_all(fanned, NARROW, 0, 0, tiled=True)  12.5 us
    all_to_all x1, blocking collectives, per_device(): lax.all_to_all(jnp.concatenate([copies, link], axis=1), 'z', 0, 0, tiled=...  10.8 us
    ppermute x1, starting transfers between devices, per_device(): back = lax.ppermute(away, 'core', [(0, 1), (1, 0)])  5.61 us
  transfers between devices with their start and end apart: 1, of which 1 were waited for; matrix products, arithmetic and copies ran while one was open for 0% of the time, Pallas kernels for 1%

profile of v4, /device:TPU:1, one launch (start us, length us, event | category | flops | bytes accessed | tf_op | source)
XLA Modules:
  0.0 156.8 jit_solution(7557839737136196196)
XLA Ops:
  0.7 2.0 %copy.9 = bf16[256,8,4,128]{3,1,2,0:T(8,128)(2,1)S(1)} copy(bf16[256,8,4,128]{3,2,1,0:T(4,128)(2,1)} %bitcast.28) | data formatting | bytes 4194304
  2.8 20.0 %all_to_all.50.packed_ref = bf16[8,192,128]{2,1,0:T(8,128)(2,1)S(1)} all-to-all(bf16[8,192,128]{2,1,0:T(8,128)(2,1)S(1)} %pack.1), channel_id=1, replica_groups=mesh['y'=8,'z'=8,'x'=4,'core'=2] {'y'}, dimensions={0} | all-to-all | bytes 786432 | tf_op jit(solution)/shard_map/all_to_all | solution.py:273
  23.0 12.4 %all_to_all.51 = bf16[8,64,128]{2,1,0:T(8,128)(2,1)S(1)} all-to-all(bf16[8,64,128]{2,1,0:T(8,128)(2,1)S(1)} %broadcast_in_dim.23), channel_id=1, replica_groups=mesh['y'=8,'z'=8,'x'=4,'core'=2] {'x','core'}, dimensions={0} | all-to-all | bytes 262144 | tf_op jit(solution)/shard_map/all_to_all | solution.py:28
  35.4 0.1 convolution_convert_fusion.3
  35.6 17.9 %all_to_all.52 = bf16[8,80,128]{2,1,0:T(8,128)(2,1)S(1)} all-to-all(bf16[8,80,128]{2,1,0:T(8,128)(2,1)S(1)} %broadcast_in_dim.24), channel_id=1, replica_groups=mesh['y'=8,'z'=8,'x'=4,'core'=2] {'z'}, dimensions={0} | all-to-all | bytes 327680 | tf_op jit(solution)/shard_map/all_to_all | solution.py:28
  53.5 0.1 fusion
  53.7 0.1 convolution_convert_fusion.1
  53.9 13.1 %all_to_all.53 = bf16[8,192,128]{2,1,0:T(8,128)(2,1)S(1)} all-to-all(bf16[8,192,128]{2,1,0:T(8,128)(2,1)S(1)} %broadcast_in_dim.25), channel_id=1, replica_groups=mesh['y'=8,'z'=8,'x'=4,'core'=2] {'x','core'}, dimensions={0} | all-to-all | bytes 786432 | tf_op jit(solution)/shard_map/all_to_all | solution.py:28
  67.1 0.1 convolution_convert_fusion.2
  67.2 0.2 convolution_convert_fusion
  67.4 10.8 %all_to_all.54 = bf16[8,80,128]{2,1,0:T(8,128)(2,1)S(1)} all-to-all(bf16[8,80,128]{2,1,0:T(8,128)(2,1)S(1)} %pad_maximum_fusion), channel_id=1, replica_groups=mesh['y'=8,'z'=8,'x'=4,'core'=2] {'z'}, dimensions={0} | all-to-all | bytes 327680 | tf_op jit(solution)/shard_map/all_to_all | solution.py:299
  78.3 12.2 %all_to_all.55._.early_ref = bf16[8,144,128]{2,1,0:T(8,128)(2,1)S(1)} all-to-all(bf16[8,144,128]{2,1,0:T(8,128)(2,1)S(1)} %broadcast_in_dim.53), channel_id=1, replica_groups=mesh['y'=8,'z'=8,'x'=4,'core'=2] {'y'}, dimensions={0} | all-to-all | bytes 589824 | tf_op jit(solution)/shard_map/all_to_all | solution.py:28
  90.5 0.2 fan.1
  90.7 12.5 %all_to_all.56.fanned_ref = bf16[8,64,256]{2,1,0:T(8,128)(2,1)S(1)} all-to-all(bf16[8,64,256]{2,1,0:T(8,128)(2,1)S(1)} %fan.1), channel_id=1, replica_groups=mesh['y'=8,'z'=8,'x'=4,'core'=2] {'x','core'}, dimensions={0} | all-to-all | bytes 524288 | tf_op jit(solution)/shard_map/all_to_all | solution.py:307
  103.2 0.2 pair.1
  103.4 12.6 %all_to_all.57 = bf16[8,64,256]{2,1,0:T(8,128)(2,1)S(1)} all-to-all(bf16[8,64,256]{2,1,0:T(8,128)(2,1)S(1)} %pair.1), channel_id=1, replica_groups=mesh['y'=8,'z'=8,'x'=4,'core'=2] {'z'}, dimensions={0} | all-to-all | bytes 524288 | tf_op jit(solution)/shard_map/all_to_all | solution.py:309
  116.1 11.8 %all_to_all.58.late_ref = bf16[8,64,256]{2,1,0:T(8,128)(2,1)S(1)} all-to-all(bf16[8,64,256]{2,1,0:T(8,128)(2,1)S(1)} %broadcast_in_dim.54), channel_id=1, replica_groups=mesh['y'=8,'z'=8,'x'=4,'core'=2] {'y'}, dimensions={0} | all-to-all | bytes 524288 | tf_op jit(solution)/shard_map/all_to_all | solution.py:28
  127.9 1.4 product.2
  129.3 5.6 %collective-permute-start = (bf16[4,256,512]{2,1,0:T(8,128)(2,1)S(1)}, bf16[4,256,512]{2,1,0:T(8,128)(2,1)S(1)}, u32[]{:S(2)}, u32[]{:S(2)}) collective-permute-start(bf16[4,256,512]{2,1,0:T(8,128)(2,1)S(1)} %product.2), channel_id=1, source_target_pairs={{0,1},{1,0},{2,3},{3,2},{4,5},{5,4},{6,7},{7,6},{8,9},{9,8},{10,11... | collective-permute-start | bytes 3145736 | tf_op jit(solution)/shard_map/ppermute | solution.py:314
  134.9 1.0 turn.1.refs_1_
  135.9 1.3 collective-permute-done.refs_0_
  137.2 1.4 product.3
  138.6 17.2 %all_to_all.59 = bf16[4,256,512]{2,1,0:T(8,128)(2,1)S(1)} all-to-all(bf16[4,256,512]{2,1,0:T(8,128)(2,1)S(1)} %product.3), channel_id=1, replica_groups=mesh['y'=8,'z'=8,'x'=4,'core'=2] {'x'}, dimensions={0} | all-to-all | bytes 2097152 | tf_op jit(solution)/shard_map/all_to_all | solution.py:317
  155.9 0.9 convert_reduce_fusion
  (27 shorter events, 0.6 us)
Async XLA Ops:
  0.6 2.1 %copy-start = (f32[1,4,16,512]{3,2,1,0:T(8,128)S(1)}, f32[1,4,16,512]{3,2,1,0:T(8,128)}, u32[]{:S(2)}) copy-start(f32[1,4,16,512]{3,2,1,0:T(8,128)} %partial_ref.1) | copy-start | bytes 393220
  0.7 2.1 %copy-start.1 = (bf16[4,16,128]{2,1,0:T(8,128)(2,1)S(1)}, bf16[4,16,128]{2,1,0:T(8,128)(2,1)}, u32[]{:S(2)}) copy-start(bf16[4,16,128]{2,1,0:T(8,128)(2,1)} %native_ref.1) | copy-start | bytes 49156
  0.7 2.1 %copy-start.2 = (bf16[4,16,512]{2,1,0:T(8,128)(2,1)S(1)}, bf16[4,16,512]{2,1,0:T(8,128)(2,1)}, u32[]{:S(2)}) copy-start(bf16[4,16,512]{2,1,0:T(8,128)(2,1)} %right_ref.1) | copy-start | bytes 196612
  0.7 2.1 %copy-start.3 = (bf16[4,16,4,128]{3,2,1,0:T(4,128)(2,1)S(1)}, bf16[4,16,4,128]{3,2,1,0:T(4,128)(2,1)}, u32[]{:S(2)}) copy-start(bf16[4,16,4,128]{3,2,1,0:T(4,128)(2,1)} %window_ref.1) | copy-start | bytes 196612
  129.3 7.9 %collective-permute-start = (bf16[4,256,512]{2,1,0:T(8,128)(2,1)S(1)}, bf16[4,256,512]{2,1,0:T(8,128)(2,1)S(1)}, u32[]{:S(2)}, u32[]{:S(2)}) collective-permute-start(bf16[4,256,512]{2,1,0:T(8,128)(2,1)S(1)} %product.2), channel_id=1, source_target_pairs={{0,1},{1,0},{2,3},{3,2},{4,5},{5,4},{6,7},{7,6},{8,9},{9,8},{10,11... | collective-permute-start | bytes 3145736 | tf_op jit(solution)/shard_map/ppermute | solution.py:314

commit v5 on v4

--- a/solution.py
+++ b/solution.py
@@ -16,6 +16,7 @@
 ROWS_T = (((1,), (1,)), ((), ()))
 VMEM = pl.BlockSpec(memory_space=pltpu.VMEM)
 ANY = pl.BlockSpec(memory_space=pl.ANY)
+HBM = pl.BlockSpec(memory_space=pltpu.HBM)
 SMEM = pl.BlockSpec(memory_space=pltpu.SMEM)
 
 
@@ -36,7 +37,7 @@
     return [(block, prior) for block in range(steps) for prior in range(block)]
 
 
-def pack(right_side, partial_in, window_factor, inverse_t, first, ahead):
+def pack(right_side, partial_in, window_factor, inverse_t, first):
     steps, rows, rhs = right_side.shape
     cols = inverse_t.shape[2]
     part = rhs // NUM_Y
@@ -44,7 +45,18 @@
     split = (len(pairs) + steps) * rows
     half = steps // 2
 
-    def body(first_ref, right_ref, partial_ref, window_ref, inverse_ref, _, out_ref):
+    def body(first_ref, *refs):
+        sources, (out_ref, own_ref), held, sems = refs[:4], refs[4:6], refs[6:10], refs[10]
+        loads = [
+            pltpu.make_async_copy(source, target, sems.at[i])
+            for i, (source, target) in enumerate(zip(sources, held))
+        ]
+        for load in loads:
+            load.start()
+        for load in loads:
+            load.wait()
+        right_ref, partial_ref, window_ref, inverse_ref = held
+        own_ref[...] = inverse_ref[2]
         for spot, (block, prior) in enumerate(pairs):
             piece = window_ref[block].astype(F32)[:, prior, :].astype(BF16)
             for y in range(NUM_Y):
@@ -69,25 +81,35 @@
 
     return pl.pallas_call(
         body,
-        in_specs=[SMEM, VMEM, VMEM, VMEM, VMEM, ANY],
-        out_specs=VMEM,
-        out_shape=pltpu.VMEM((NUM_Y, split + half * rows, cols), BF16),
+        in_specs=[SMEM] + [HBM] * 4,
+        out_specs=[VMEM] * 2,
+        out_shape=[
+            pltpu.VMEM((NUM_Y, split + half * rows, cols), BF16),
+            pltpu.VMEM((rows, cols), BF16),
+        ],
+        scratch_shapes=[
+            pltpu.VMEM(array.shape, array.dtype)
+            for array in (right_side, partial_in, window_factor, inverse_t)
+        ]
+        + [pltpu.SemaphoreType.DMA((4,))],
         compiler_params=pltpu.CompilerParams(vmem_limit_bytes=SCRATCH),
         name="pack",
-    )(first, right_side, partial_in, window_factor, inverse_t, ahead)
-
-
-def unpack(packed, native, rows, part):
+    )(
+        first,
+        *(
+            pltpu.with_memory_space_constraint(array, pltpu.HBM)
+            for array in (right_side, partial_in, window_factor, inverse_t)
+        ),
+    )
+
+
+def unpack(packed, rows, part):
     cols = packed.shape[2]
     slab = NUM_Y * rows
     pairs = pairs_of(STEPS)
     split = (len(pairs) + STEPS) * rows
 
-    def body(
-        packed_ref, native_ref, early_ref, late_ref, inverse_ref,
-        one_ref, two_ref, last_ref, own_ref,
-    ):
-        own_ref[...] = native_ref[2]
+    def body(packed_ref, early_ref, late_ref, inverse_ref, one_ref, two_ref, last_ref):
         target = {
             (1, 0): (one_ref, 0, 0),
             (2, 0): (two_ref, 0, 0),
@@ -124,22 +146,21 @@
         pltpu.VMEM((slab, cols), BF16),
         pltpu.VMEM((2 * slab, 2 * cols), BF16),
         pltpu.VMEM((slab, cols), BF16),
-        pltpu.VMEM((rows, cols), BF16),
     ]
     return pl.pallas_call(
         body,
-        in_specs=[VMEM, VMEM],
+        in_specs=[VMEM],
         out_specs=[VMEM] * len(outs),
         out_shape=outs,
         compiler_params=pltpu.CompilerParams(vmem_limit_bytes=SCRATCH),
         name="unpack",
-    )(*resident(packed, native))
-
-
-def fan(terms, solved, window, ahead):
+    )(*resident(packed))
+
+
+def fan(terms, solved, window):
     part, cols = terms.shape[0], solved.shape[1]
 
-    def body(terms_ref, solved_ref, window_ref, _, out_ref):
+    def body(terms_ref, solved_ref, window_ref, out_ref):
         value = terms_ref[...]
         for block in range(2):
             value = value + lax.dot_general(
@@ -147,18 +168,16 @@
                 window_ref[:, block * cols : (block + 1) * cols],
                 ROWS_T, preferred_element_type=F32,
             )
-        value = value.astype(BF16)
-        for n in range(NUM_NARROW):
-            out_ref[n] = value
-
-    return pl.pallas_call(
-        body,
-        in_specs=[VMEM] * 3 + [ANY],
+        out_ref[...] = value.astype(BF16)
+
+    return pl.pallas_call(
+        body,
+        in_specs=[VMEM] * 3,
         out_specs=VMEM,
-        out_shape=pltpu.VMEM((NUM_NARROW,) + terms.shape, BF16),
+        out_shape=pltpu.VMEM(terms.shape, BF16),
         compiler_params=pltpu.CompilerParams(vmem_limit_bytes=SCRATCH),
         name="fan",
-    )(*resident(terms, solved, window), ahead)
+    )(*resident(terms, solved, window))
 
 
 def pair(fanned, inverse, early):
@@ -226,7 +245,8 @@
 
 
 def product(core, factor, early, late, back=None):
-    trail_rows, depth = factor.shape
+    trail_rows, steps, cols = factor.shape
+    depth = steps * cols
     rhs = NUM_Y * late.shape[1]
     own = trail_rows // NUM_NARROW
 
@@ -235,16 +255,21 @@
         side = 1 - core_ref[0] if back is None else core_ref[0]
         flatten(early_ref, late_ref, flat_ref)
 
-        @pl.loop(0, NUM_X)
-        def _(i):
-            row = pl.multiple_of((NUM_CORE * i + side) * own, own)
+        def rows_of(start, i):
             value = lax.dot_general(
-                factor_ref[pl.ds(row, own), :], flat_ref[...], ROWS_T,
-                preferred_element_type=F32,
+                factor_ref[start : start + own].reshape(own, depth), flat_ref[...],
+                ROWS_T, preferred_element_type=F32,
             )
             if back is not None:
                 value = value + refs[0][i].astype(F32)
             out_ref[i] = value.astype(BF16)
+
+        for half in range(NUM_CORE):
+
+            @pl.when(side == half)
+            def _():
+                for i in range(NUM_X):
+                    rows_of((NUM_CORE * i + half) * own, i)
 
     arrays = resident(factor, early, late) + ([] if back is None else resident(back[0]))
     after = []
@@ -268,11 +293,10 @@
     trail_rows = trailing_factor.shape[0]
 
     first = (lax.axis_index(NARROW) == 0).astype(F32)[None]
-    flat_factor = trailing_factor.reshape(trail_rows, steps * cols)
-    packed = pack(right_side, partial_in, window_factor, inverse_t, first, flat_factor)
+    packed, own = pack(right_side, partial_in, window_factor, inverse_t, first)
     packed = lax.all_to_all(packed, "y", 0, 0, tiled=True)
-    first_terms, late_terms, inverse, window_one, window_two, window_last, own = unpack(
-        packed, inverse_t, rows, part
+    first_terms, late_terms, inverse, window_one, window_two, window_last = unpack(
+        packed, rows, part
     )
 
     def over_narrow(value):
@@ -303,17 +327,16 @@
 
     stack = jnp.concatenate([solved_0, got])
     early = spread(stack, "y", NUM_Y)
-    fanned = fan(late_terms, stack, window_two, early)
-    fanned = lax.all_to_all(fanned, NARROW, 0, 0, tiled=True)
+    fanned = lax.all_gather(fan(late_terms, stack, window_two), NARROW, axis=0)
     share = pair(fanned, inverse, early)
     late = total(lax.all_to_all(share, "z", 0, 0, tiled=True)).astype(BF16)
     late = spread(late, "y", NUM_Y)
 
     core = lax.axis_index("core").astype(jnp.int32)[None]
-    away = product(core, flat_factor, early, late)
+    away = product(core, trailing_factor, early, late)
     back = lax.ppermute(away, "core", [(0, 1), (1, 0)])
     solved = turn(early, late)
-    kept = product(core, flat_factor, early, late, (back, solved))
+    kept = product(core, trailing_factor, early, late, (back, solved))
     trailing = total(lax.all_to_all(kept, "x", 0, 0, tiled=True))
     return (solved, trailing)
 

time: 157 us -> 156 us (level)
  blocking collectives: 141 us -> 139 us
  starting transfers between devices: 5.61 us -> 7.35 us
    all_gather x0 -> x1, blocking collectives: none -> 15 us  [per_device(): fanned = lax.all_gather(fan(late_terms, stack, window_two), NARROW, axis=0)]
    all_to_all x1 -> x0, blocking collectives: 12.5 us -> none  [per_device(): fanned = lax.all_to_all(fanned, NARROW, 0, 0, tiled=True)]
    all_to_all x5 -> x4, blocking collectives: 67.5 us -> 60.9 us  [spread(): return lax.all_to_all(copies, axis, 0, 0, tiled=True)]
    all_to_all x0 -> x1, starting transfers between devices: none -> 3.42 us  [spread(): return lax.all_to_all(copies, axis, 0, 0, tiled=True)]
    all_to_all x1, blocking collectives: 12.6 us -> 14.8 us  [per_device(): late = total(lax.all_to_all(share, 'z', 0, 0, tiled=True)).astype(BF16)]
    unnamed x9 -> x2, local copies, waits for them, and re-layouts: 2.03 us -> 0.01 us
    ppermute x1, starting transfers between devices: 5.61 us -> 3.93 us  [per_device(): back = lax.ppermute(away, 'core', [(0, 1), (1, 0)])]
  transfers between devices with their start and end apart: 1 -> 2, of which waited for: 1 -> 1; matrix products, arithmetic and copies ran while one was open for 0% -> 0% of each run, Pallas kernels for 1% -> 1%
where the time goes in v5:
time: 156 us; the launch traced here: 155 us
  blocking collectives  139 us (89%)
  starting transfers between devices  7.35 us (5%)
  Pallas kernels  4.5 us (3%)
    all_to_all x4, blocking collectives, spread(): return lax.all_to_all(copies, axis, 0, 0, tiled=True)  60.9 us
    all_to_all x1, blocking collectives, per_device(): packed = lax.all_to_all(packed, 'y', 0, 0, tiled=True)  20 us
    all_to_all x1, blocking collectives, per_device(): trailing = total(lax.all_to_all(kept, 'x', 0, 0, tiled=True))  17.1 us
    all_gather x1, blocking collectives, per_device(): fanned = lax.all_gather(fan(late_terms, stack, window_two), NARROW, axis=0)  15 us
    all_to_all x1, blocking collectives, per_device(): late = total(lax.all_to_all(share, 'z', 0, 0, tiled=True)).astype(BF16)  14.8 us
    all_to_all x1, blocking collectives, per_device(): lax.all_to_all(jnp.concatenate([copies, link], axis=1), 'z', 0, 0, tiled=...  10.8 us
    ppermute x1, starting transfers between devices, per_device(): back = lax.ppermute(away, 'core', [(0, 1), (1, 0)])  3.93 us
    all_to_all x1, starting transfers between devices, spread(): return lax.all_to_all(copies, axis, 0, 0, tiled=True)  3.42 us
  transfers between devices with their start and end apart: 2, of which 1 were waited for; matrix products, arithmetic and copies ran while one was open for 0% of the time, Pallas kernels for 1%

profile of v5, /device:TPU:1, one launch (start us, length us, event | category | flops | bytes accessed | tf_op | source)
XLA Modules:
  0.0 155.3 jit_solution(5458105467744132560)
XLA Ops:
  0.6 1.1 pack.1
  1.8 20.0 %all_to_all.45.packed_ref = bf16[8,192,128]{2,1,0:T(8,128)(2,1)S(1)} all-to-all(bf16[8,192,128]{2,1,0:T(8,128)(2,1)S(1)} %get-tuple-element.10), channel_id=1, replica_groups=mesh['y'=8,'z'=8,'x'=4,'core'=2] {'y'}, dimensions={0} | all-to-all | bytes 786432 | tf_op jit(solution)/shard_map/all_to_all | solution.py:297
  21.9 12.4 %all_to_all.46 = bf16[8,64,128]{2,1,0:T(8,128)(2,1)S(1)} all-to-all(bf16[8,64,128]{2,1,0:T(8,128)(2,1)S(1)} %broadcast_in_dim.23), channel_id=1, replica_groups=mesh['y'=8,'z'=8,'x'=4,'core'=2] {'x','core'}, dimensions={0} | all-to-all | bytes 262144 | tf_op jit(solution)/shard_map/all_to_all | solution.py:29
  34.4 0.1 convolution_convert_fusion.3
  34.5 17.9 %all_to_all.47 = bf16[8,80,128]{2,1,0:T(8,128)(2,1)S(1)} all-to-all(bf16[8,80,128]{2,1,0:T(8,128)(2,1)S(1)} %broadcast_in_dim.24), channel_id=1, replica_groups=mesh['y'=8,'z'=8,'x'=4,'core'=2] {'z'}, dimensions={0} | all-to-all | bytes 327680 | tf_op jit(solution)/shard_map/all_to_all | solution.py:29
  52.4 0.1 fusion
  52.6 0.1 convolution_convert_fusion.1
  52.8 13.1 %all_to_all.48 = bf16[8,192,128]{2,1,0:T(8,128)(2,1)S(1)} all-to-all(bf16[8,192,128]{2,1,0:T(8,128)(2,1)S(1)} %broadcast_in_dim.25), channel_id=1, replica_groups=mesh['y'=8,'z'=8,'x'=4,'core'=2] {'x','core'}, dimensions={0} | all-to-all | bytes 786432 | tf_op jit(solution)/shard_map/all_to_all | solution.py:29
  66.1 0.2 convolution_convert_fusion
  66.4 10.8 %all_to_all.49 = bf16[8,80,128]{2,1,0:T(8,128)(2,1)S(1)} all-to-all(bf16[8,80,128]{2,1,0:T(8,128)(2,1)S(1)} %pad_maximum_fusion), channel_id=1, replica_groups=mesh['y'=8,'z'=8,'x'=4,'core'=2] {'z'}, dimensions={0} | all-to-all | bytes 327680 | tf_op jit(solution)/shard_map/all_to_all | solution.py:323
  77.2 0.8 broadcast_in_dim.53
  77.9 3.4 %all-to-all-start.5 = ((bf16[8,144,128]{2,1,0:T(8,128)(2,1)}), bf16[8,144,128]{2,1,0:T(8,128)(2,1)S(1)}, u32[]{:S(2)}, u32[]{:S(2)}) async-start(bf16[8,144,128]{2,1,0:T(8,128)(2,1)} %broadcast_in_dim.53), calls=%async_computation.5 | async-start | bytes 589824 | tf_op jit(solution)/shard_map/all_to_all | solution.py:29
  81.4 0.2 fan.1
  81.5 15.0 %all-gather = bf16[512,256]{1,0:T(8,128)(2,1)S(1)} all-gather(bf16[64,256]{1,0:T(8,128)(2,1)S(1)} %fan.1), channel_id=2, replica_groups=mesh['y'=8,'z'=8,'x'=4,'core'=2] {'x','core'}, dimensions={0}, use_global_device_ids=true | all-gather | bytes 294912 | tf_op jit(solution)/shard_map/all_gather | solution.py:330
  96.6 0.2 pair.1
  96.7 14.8 %all_to_all.50 = bf16[8,64,256]{2,1,0:T(8,128)(2,1)S(1)} all-to-all(bf16[8,64,256]{2,1,0:T(8,128)(2,1)S(1)} %pair.1), channel_id=1, replica_groups=mesh['y'=8,'z'=8,'x'=4,'core'=2] {'z'}, dimensions={0} | all-to-all | bytes 524288 | tf_op jit(solution)/shard_map/all_to_all | solution.py:332
  111.6 17.4 %all_to_all.51.late_ref = bf16[8,64,256]{2,1,0:T(8,128)(2,1)S(1)} all-to-all(bf16[8,64,256]{2,1,0:T(8,128)(2,1)S(1)} %broadcast_in_dim.54), channel_id=1, replica_groups=mesh['y'=8,'z'=8,'x'=4,'core'=2] {'y'}, dimensions={0} | all-to-all | bytes 524288 | tf_op jit(solution)/shard_map/all_to_all | solution.py:29
  129.0 0.9 product.2
  130.0 3.9 %collective-permute-start = (bf16[4,256,512]{2,1,0:T(8,128)(2,1)S(1)}, bf16[4,256,512]{2,1,0:T(8,128)(2,1)S(1)}, u32[]{:S(2)}, u32[]{:S(2)}) collective-permute-start(bf16[4,256,512]{2,1,0:T(8,128)(2,1)S(1)} %product.2), channel_id=1, source_target_pairs={{0,1},{1,0},{2,3},{3,2},{4,5},{5,4},{6,7},{7,6},{8,9},{9,8},{10,11... | collective-permute-start | bytes 3145736 | tf_op jit(solution)/shard_map/ppermute | solution.py:337
  133.9 1.0 turn.1.refs_1_
  134.9 1.3 collective-permute-done.refs_0_
  136.2 1.0 product.3
  137.2 17.1 %all_to_all.52 = bf16[4,256,512]{2,1,0:T(8,128)(2,1)S(1)} all-to-all(bf16[4,256,512]{2,1,0:T(8,128)(2,1)S(1)} %product.3), channel_id=1, replica_groups=mesh['y'=8,'z'=8,'x'=4,'core'=2] {'x'}, dimensions={0} | all-to-all | bytes 2097152 | tf_op jit(solution)/shard_map/all_to_all | solution.py:340
  154.3 0.9 convert_reduce_fusion
  (21 shorter events, 0.6 us)
Async XLA Ops:
  77.2 51.9 %copy-start = (bf16[2048,4,128]{2,1,0:T(4,128)(2,1)S(1)}, bf16[2048,4,128]{2,1,0:T(4,128)(2,1)}, u32[]{:S(2)}) copy-start(bf16[2048,4,128]{2,1,0:T(4,128)(2,1)} %factor_ref.3) | copy-start | bytes 6291460
  77.9 18.6 %all-to-all-start.5 = ((bf16[8,144,128]{2,1,0:T(8,128)(2,1)}), bf16[8,144,128]{2,1,0:T(8,128)(2,1)S(1)}, u32[]{:S(2)}, u32[]{:S(2)}) async-start(bf16[8,144,128]{2,1,0:T(8,128)(2,1)} %broadcast_in_dim.53), calls=%async_computation.5 | async-start | bytes 589824 | tf_op jit(solution)/shard_map/all_to_all | solution.py:29
  130.0 6.2 %collective-permute-start = (bf16[4,256,512]{2,1,0:T(8,128)(2,1)S(1)}, bf16[4,256,512]{2,1,0:T(8,128)(2,1)S(1)}, u32[]{:S(2)}, u32[]{:S(2)}) collective-permute-start(bf16[4,256,512]{2,1,0:T(8,128)(2,1)S(1)} %product.2), channel_id=1, source_target_pairs={{0,1},{1,0},{2,3},{3,2},{4,5},{5,4},{6,7},{7,6},{8,9},{9,8},{10,11... | collective-permute-start | bytes 3145736 | tf_op jit(solution)/shard_map/ppermute | solution.py:337

commit v6 on v5

--- a/solution.py
+++ b/solution.py
@@ -12,10 +12,10 @@
 NUM_Y, NUM_Z, NUM_X, NUM_CORE = 8, 8, 4, 2
 NUM_NARROW = NUM_X * NUM_CORE
 STEPS = 4
+SENT = (0, 1, 3)
 SCRATCH = 8 * 2**20
 ROWS_T = (((1,), (1,)), ((), ()))
 VMEM = pl.BlockSpec(memory_space=pltpu.VMEM)
-ANY = pl.BlockSpec(memory_space=pl.ANY)
 HBM = pl.BlockSpec(memory_space=pltpu.HBM)
 SMEM = pl.BlockSpec(memory_space=pltpu.SMEM)
 
@@ -42,7 +42,7 @@
     cols = inverse_t.shape[2]
     part = rhs // NUM_Y
     pairs = pairs_of(steps)
-    split = (len(pairs) + steps) * rows
+    split = (len(pairs) + len(SENT)) * rows
     half = steps // 2
 
     def body(first_ref, *refs):
@@ -61,8 +61,7 @@
             piece = window_ref[block].astype(F32)[:, prior, :].astype(BF16)
             for y in range(NUM_Y):
                 out_ref[y, spot * rows : (spot + 1) * rows, :] = piece
-        for block in range(steps):
-            spot = len(pairs) + block
+        for spot, block in enumerate(SENT, len(pairs)):
             piece = inverse_ref[block]
             for y in range(NUM_Y):
                 out_ref[y, spot * rows : (spot + 1) * rows, :] = piece
@@ -107,7 +106,7 @@
     cols = packed.shape[2]
     slab = NUM_Y * rows
     pairs = pairs_of(STEPS)
-    split = (len(pairs) + STEPS) * rows
+    split = (len(pairs) + len(SENT)) * rows
 
     def body(packed_ref, early_ref, late_ref, inverse_ref, one_ref, two_ref, last_ref):
         target = {
@@ -124,7 +123,7 @@
                 ref[row + y * rows : row + (y + 1) * rows, col : col + cols] = (
                     packed_ref[y, spot * rows : (spot + 1) * rows, :]
                 )
-        for block in range(STEPS):
+        for block in range(len(SENT)):
             spot = len(pairs) + block
             for y in range(NUM_Y):
                 inverse_ref[block, y * rows : (y + 1) * rows, :] = packed_ref[
@@ -142,7 +141,7 @@
     outs = [
         pltpu.VMEM((2, part, slab), F32),
         pltpu.VMEM((part, 2 * slab), F32),
-        pltpu.VMEM((STEPS, slab, cols), BF16),
+        pltpu.VMEM((len(SENT), slab, cols), BF16),
         pltpu.VMEM((slab, cols), BF16),
         pltpu.VMEM((2 * slab, 2 * cols), BF16),
         pltpu.VMEM((slab, cols), BF16),
@@ -191,11 +190,14 @@
             residue = residue + fanned_ref[n].astype(F32)
         residue = (-residue).astype(BF16)
         two, three = residue[:, :slab], residue[:, slab:]
-        link = jnp.concatenate(
-            [early_ref[y, 2 * part : 2 * part + rows, :] for y in range(NUM_Y)], axis=0
+        link, second = (
+            jnp.concatenate(
+                [early_ref[y, start : start + rows, :] for y in range(NUM_Y)], axis=0
+            )
+            for start in (2 * part, 2 * part + rows)
         )
-        left = jnp.dot(two, inverse_ref[2], preferred_element_type=F32)
-        right = jnp.dot(three, inverse_ref[3], preferred_element_type=F32)
+        left = jnp.dot(two, second, preferred_element_type=F32)
+        right = jnp.dot(three, inverse_ref[2], preferred_element_type=F32)
         right = right + jnp.dot(two, link, preferred_element_type=F32)
         for z in range(NUM_Z):
             out_ref[z, :, :cols] = left.astype(BF16)
@@ -244,46 +246,50 @@
     )(*resident(early, late))
 
 
-def product(core, factor, early, late, back=None):
+def product(core, factor, early, late, dtype):
     trail_rows, steps, cols = factor.shape
     depth = steps * cols
     rhs = NUM_Y * late.shape[1]
     own = trail_rows // NUM_NARROW
 
-    def body(core_ref, factor_ref, early_ref, late_ref, *refs):
-        out_ref, flat_ref = refs[-2:]
-        side = 1 - core_ref[0] if back is None else core_ref[0]
+    def body(core_ref, factor_ref, early_ref, late_ref, out_ref, flat_ref):
+        side = 1 - core_ref[0] if dtype == BF16 else core_ref[0]
         flatten(early_ref, late_ref, flat_ref)
-
-        def rows_of(start, i):
-            value = lax.dot_general(
-                factor_ref[start : start + own].reshape(own, depth), flat_ref[...],
-                ROWS_T, preferred_element_type=F32,
-            )
-            if back is not None:
-                value = value + refs[0][i].astype(F32)
-            out_ref[i] = value.astype(BF16)
-
         for half in range(NUM_CORE):
 
             @pl.when(side == half)
             def _():
                 for i in range(NUM_X):
-                    rows_of((NUM_CORE * i + half) * own, i)
-
-    arrays = resident(factor, early, late) + ([] if back is None else resident(back[0]))
-    after = []
-    if back is not None:
-        after = [pltpu.with_memory_space_constraint(back[1], pltpu.HBM)]
-    return pl.pallas_call(
-        body,
-        in_specs=[SMEM] + [VMEM] * len(arrays) + [ANY] * len(after),
+                    start = (NUM_CORE * i + half) * own
+                    out_ref[i] = lax.dot_general(
+                        factor_ref[start : start + own].reshape(own, depth),
+                        flat_ref[...], ROWS_T, preferred_element_type=F32,
+                    ).astype(dtype)
+
+    return pl.pallas_call(
+        body,
+        in_specs=[SMEM] + [VMEM] * 3,
         out_specs=VMEM,
         scratch_shapes=[pltpu.VMEM((rhs, depth), BF16)],
-        out_shape=pltpu.VMEM((NUM_X, own, rhs), BF16),
+        out_shape=pltpu.VMEM((NUM_X, own, rhs), dtype),
         compiler_params=pltpu.CompilerParams(vmem_limit_bytes=SCRATCH),
         name="product",
-    )(core, *arrays, *after)
+    )(core, *resident(factor, early, late))
+
+
+def merge(kept, back, ahead):
+    def body(kept_ref, back_ref, _, out_ref):
+        for i in range(NUM_X):
+            out_ref[i] = (kept_ref[i] + back_ref[i].astype(F32)).astype(BF16)
+
+    return pl.pallas_call(
+        body,
+        in_specs=[VMEM, VMEM, HBM],
+        out_specs=VMEM,
+        out_shape=pltpu.VMEM(kept.shape, BF16),
+        compiler_params=pltpu.CompilerParams(vmem_limit_bytes=SCRATCH),
+        name="merge",
+    )(*resident(kept, back), pltpu.with_memory_space_constraint(ahead, pltpu.HBM))
 
 
 def per_device(right_side, partial_in, window_factor, inverse_t, trailing_factor):
@@ -316,7 +322,7 @@
     residue, link = (-both[:part]).astype(BF16), (-both[part:]).astype(BF16)
     share = jnp.dot(residue, inverse[1], preferred_element_type=F32).astype(BF16)
     link = lax.dot_general(
-        link, inverse[3], (((0,), (0,)), ((), ())), preferred_element_type=F32
+        link, inverse[2], (((0,), (0,)), ((), ())), preferred_element_type=F32
     )
     copies = jnp.broadcast_to(share[None], (NUM_Z,) + share.shape)
     link = link.astype(BF16).reshape(NUM_Z, rows, cols)
@@ -325,7 +331,7 @@
     )
     got = total(got).astype(BF16)
 
-    stack = jnp.concatenate([solved_0, got])
+    stack = jnp.concatenate([solved_0, got, own])
     early = spread(stack, "y", NUM_Y)
     fanned = lax.all_gather(fan(late_terms, stack, window_two), NARROW, axis=0)
     share = pair(fanned, inverse, early)
@@ -333,10 +339,11 @@
     late = spread(late, "y", NUM_Y)
 
     core = lax.axis_index("core").astype(jnp.int32)[None]
-    away = product(core, trailing_factor, early, late)
+    away = product(core, trailing_factor, early, late, BF16)
     back = lax.ppermute(away, "core", [(0, 1), (1, 0)])
+    kept = product(core, trailing_factor, early, late, F32)
     solved = turn(early, late)
-    kept = product(core, trailing_factor, early, late, (back, solved))
+    kept = merge(kept, back, solved)
     trailing = total(lax.all_to_all(kept, "x", 0, 0, tiled=True))
     return (solved, trailing)
 

time: 156 us -> 154 us (0.987)
  no operation moved by 1% of the time
where the time goes in v6:
time: 154 us
  blocking collectives  138 us (90%)
  starting transfers between devices  7.36 us (5%)
  Pallas kernels  4.65 us (3%)
    all_to_all x4, blocking collectives, spread(): return lax.all_to_all(copies, axis, 0, 0, tiled=True)  61.2 us
    all_to_all x1, blocking collectives, per_device(): packed = lax.all_to_all(packed, 'y', 0, 0, tiled=True)  18.9 us
    all_to_all x1, blocking collectives, per_device(): trailing = total(lax.all_to_all(kept, 'x', 0, 0, tiled=True))  17.1 us
    all_gather x1, blocking collectives, per_device(): fanned = lax.all_gather(fan(late_terms, stack, window_two), NARROW, axis=0)  15 us
    all_to_all x1, blocking collectives, per_device(): late = total(lax.all_to_all(share, 'z', 0, 0, tiled=True)).astype(BF16)  14.8 us
    all_to_all x1, blocking collectives, per_device(): lax.all_to_all(jnp.concatenate([copies, link], axis=1), 'z', 0, 0, tiled=...  10.8 us
    ppermute x1, starting transfers between devices, per_device(): back = lax.ppermute(away, 'core', [(0, 1), (1, 0)])  3.93 us
    all_to_all x1, starting transfers between devices, spread(): return lax.all_to_all(copies, axis, 0, 0, tiled=True)  3.43 us
  transfers between devices with their start and end apart: 2, of which 1 were waited for; matrix products, arithmetic and copies ran while one was open for 0% of the time, Pallas kernels for 1%

profile of v6, /device:TPU:1, one launch (start us, length us, event | category | flops | bytes accessed | tf_op | source)
XLA Modules:
  0.0 153.8 jit_solution(13130672862697943367)
XLA Ops:
  0.6 1.1 pack.1
  1.8 18.9 %all_to_all.45.packed_ref = bf16[8,176,128]{2,1,0:T(8,128)(2,1)S(1)} all-to-all(bf16[8,176,128]{2,1,0:T(8,128)(2,1)S(1)} %get-tuple-element.10), channel_id=1, replica_groups=mesh['y'=8,'z'=8,'x'=4,'core'=2] {'y'}, dimensions={0} | all-to-all | bytes 720896 | tf_op jit(solution)/shard_map/all_to_all | solution.py:303
  20.8 12.8 %all_to_all.46 = bf16[8,64,128]{2,1,0:T(8,128)(2,1)S(1)} all-to-all(bf16[8,64,128]{2,1,0:T(8,128)(2,1)S(1)} %broadcast_in_dim.23), channel_id=1, replica_groups=mesh['y'=8,'z'=8,'x'=4,'core'=2] {'x','core'}, dimensions={0} | all-to-all | bytes 262144 | tf_op jit(solution)/shard_map/all_to_all | solution.py:29
  33.8 17.9 %all_to_all.47 = bf16[8,80,128]{2,1,0:T(8,128)(2,1)S(1)} all-to-all(bf16[8,80,128]{2,1,0:T(8,128)(2,1)S(1)} %broadcast_in_dim.24), channel_id=1, replica_groups=mesh['y'=8,'z'=8,'x'=4,'core'=2] {'z'}, dimensions={0} | all-to-all | bytes 327680 | tf_op jit(solution)/shard_map/all_to_all | solution.py:29
  51.7 0.1 fusion
  51.9 0.1 convolution_convert_fusion.1
  52.1 13.1 %all_to_all.48 = bf16[8,192,128]{2,1,0:T(8,128)(2,1)S(1)} all-to-all(bf16[8,192,128]{2,1,0:T(8,128)(2,1)S(1)} %broadcast_in_dim.25), channel_id=1, replica_groups=mesh['y'=8,'z'=8,'x'=4,'core'=2] {'x','core'}, dimensions={0} | all-to-all | bytes 786432 | tf_op jit(solution)/shard_map/all_to_all | solution.py:29
  65.4 0.2 convolution_convert_fusion
  65.7 10.8 %all_to_all.49 = bf16[8,80,128]{2,1,0:T(8,128)(2,1)S(1)} all-to-all(bf16[8,80,128]{2,1,0:T(8,128)(2,1)S(1)} %pad_maximum_fusion), channel_id=1, replica_groups=mesh['y'=8,'z'=8,'x'=4,'core'=2] {'z'}, dimensions={0} | all-to-all | bytes 327680 | tf_op jit(solution)/shard_map/all_to_all | solution.py:329
  76.5 0.8 broadcast_in_dim.53
  77.2 3.4 %all-to-all-start.5 = ((bf16[8,160,128]{2,1,0:T(8,128)(2,1)}), bf16[8,160,128]{2,1,0:T(8,128)(2,1)S(1)}, u32[]{:S(2)}, u32[]{:S(2)}) async-start(bf16[8,160,128]{2,1,0:T(8,128)(2,1)} %broadcast_in_dim.53), calls=%async_computation.5 | async-start | bytes 655360 | tf_op jit(solution)/shard_map/all_to_all | solution.py:29
  80.7 0.2 fan.1
  80.8 15.0 %all-gather = bf16[512,256]{1,0:T(8,128)(2,1)S(1)} all-gather(bf16[64,256]{1,0:T(8,128)(2,1)S(1)} %fan.1), channel_id=2, replica_groups=mesh['y'=8,'z'=8,'x'=4,'core'=2] {'x','core'}, dimensions={0}, use_global_device_ids=true | all-gather | bytes 294912 | tf_op jit(solution)/shard_map/all_gather | solution.py:336
  95.9 0.2 pair.1
  96.1 14.8 %all_to_all.50 = bf16[8,64,256]{2,1,0:T(8,128)(2,1)S(1)} all-to-all(bf16[8,64,256]{2,1,0:T(8,128)(2,1)S(1)} %pair.1), channel_id=1, replica_groups=mesh['y'=8,'z'=8,'x'=4,'core'=2] {'z'}, dimensions={0} | all-to-all | bytes 524288 | tf_op jit(solution)/shard_map/all_to_all | solution.py:338
  110.9 17.4 %all_to_all.51.late_ref = bf16[8,64,256]{2,1,0:T(8,128)(2,1)S(1)} all-to-all(bf16[8,64,256]{2,1,0:T(8,128)(2,1)S(1)} %broadcast_in_dim.54), channel_id=1, replica_groups=mesh['y'=8,'z'=8,'x'=4,'core'=2] {'y'}, dimensions={0} | all-to-all | bytes 524288 | tf_op jit(solution)/shard_map/all_to_all | solution.py:29
  128.4 0.9 product.3
  129.3 3.9 %collective-permute-start = (bf16[4,256,512]{2,1,0:T(8,128)(2,1)S(1)}, bf16[4,256,512]{2,1,0:T(8,128)(2,1)S(1)}, u32[]{:S(2)}, u32[]{:S(2)}) collective-permute-start(bf16[4,256,512]{2,1,0:T(8,128)(2,1)S(1)} %product.3), channel_id=1, source_target_pairs={{0,1},{1,0},{2,3},{3,2},{4,5},{5,4},{6,7},{7,6},{8,9},{9,8},{10,11... | collective-permute-start | bytes 3145736 | tf_op jit(solution)/shard_map/ppermute | solution.py:343
  133.2 1.0 turn.1._
  134.2 0.9 product.2.kept_ref
  135.1 0.4 collective-permute-done.back_ref
  135.5 0.3 merge.1
  135.8 17.1 %all_to_all.52 = bf16[4,256,512]{2,1,0:T(8,128)(2,1)S(1)} all-to-all(bf16[4,256,512]{2,1,0:T(8,128)(2,1)S(1)} %merge.1), channel_id=1, replica_groups=mesh['y'=8,'z'=8,'x'=4,'core'=2] {'x'}, dimensions={0} | all-to-all | bytes 2097152 | tf_op jit(solution)/shard_map/all_to_all | solution.py:347
  152.9 0.9 convert_reduce_fusion
  (22 shorter events, 0.7 us)
Async XLA Ops:
  76.5 51.9 %copy-start = (bf16[2048,4,128]{2,1,0:T(4,128)(2,1)S(1)}, bf16[2048,4,128]{2,1,0:T(4,128)(2,1)}, u32[]{:S(2)}) copy-start(bf16[2048,4,128]{2,1,0:T(4,128)(2,1)} %factor_ref.3) | copy-start | bytes 6291460
  77.2 18.6 %all-to-all-start.5 = ((bf16[8,160,128]{2,1,0:T(8,128)(2,1)}), bf16[8,160,128]{2,1,0:T(8,128)(2,1)S(1)}, u32[]{:S(2)}, u32[]{:S(2)}) async-start(bf16[8,160,128]{2,1,0:T(8,128)(2,1)} %broadcast_in_dim.53), calls=%async_computation.5 | async-start | bytes 655360 | tf_op jit(solution)/shard_map/all_to_all | solution.py:29
  129.3 6.2 %collective-permute-start = (bf16[4,256,512]{2,1,0:T(8,128)(2,1)S(1)}, bf16[4,256,512]{2,1,0:T(8,128)(2,1)S(1)}, u32[]{:S(2)}, u32[]{:S(2)}) collective-permute-start(bf16[4,256,512]{2,1,0:T(8,128)(2,1)S(1)} %product.3), channel_id=1, source_target_pairs={{0,1},{1,0},{2,3},{3,2},{4,5},{5,4},{6,7},{7,6},{8,9},{9,8},{10,11... | collective-permute-start | bytes 3145736 | tf_op jit(solution)/shard_map/ppermute | solution.py:343

commit v7 on v6

--- a/solution.py
+++ b/solution.py
@@ -156,6 +156,81 @@
     )(*resident(packed))
 
 
+def summed(ref, rows=slice(None)):
+    value = ref[0, rows, :].astype(F32)
+    for i in range(1, ref.shape[0]):
+        value = value + ref[i, rows, :].astype(F32)
+    return value
+
+
+def stage(body, outs, *arrays):
+    return pl.pallas_call(
+        body,
+        in_specs=[VMEM] * len(arrays),
+        out_specs=[VMEM] * len(outs),
+        out_shape=[pltpu.VMEM(shape, BF16) for shape in outs],
+        compiler_params=pltpu.CompilerParams(vmem_limit_bytes=SCRATCH),
+        name=body.__name__,
+    )(*resident(*arrays))
+
+
+def step_zero(fanned, inverse, own):
+    part, cols = fanned.shape[1:]
+    rows = own.shape[0]
+
+    def zero(fanned_ref, inverse_ref, own_ref, out_ref):
+        residue = (-summed(fanned_ref)).astype(BF16)
+        share = jnp.dot(residue, inverse_ref[0], preferred_element_type=F32)
+        share = share.astype(BF16)
+        for z in range(NUM_Z):
+            out_ref[z, :part, :] = share
+            out_ref[z, part:, :] = own_ref[...]
+
+    return stage(zero, [(NUM_Z, part + rows, cols)], fanned, inverse, own)[0]
+
+
+def step_one_fan(got, terms, window_one, window_last):
+    part, slab = terms.shape[1:]
+    cols = got.shape[2]
+    rows = got.shape[1] - part
+
+    def one_fan(got_ref, terms_ref, one_ref, last_ref, solved_ref, out_ref):
+        solved = summed(got_ref, slice(0, part)).astype(BF16)
+        solved_ref[...] = solved
+        ahead = jnp.concatenate(
+            [got_ref[z, part : part + rows, :] for z in range(NUM_Z)], axis=0
+        )
+        fanned = terms_ref[1] + lax.dot_general(
+            solved, one_ref[...], ROWS_T, preferred_element_type=F32
+        )
+        link = lax.dot_general(
+            last_ref[...], ahead, ROWS_T, preferred_element_type=F32
+        )
+        for n in range(NUM_NARROW):
+            out_ref[n, :part, :] = fanned.astype(BF16)
+            out_ref[n, part:, :] = link.astype(BF16)
+
+    outs = [(part, cols), (NUM_NARROW, part + slab, slab)]
+    return stage(one_fan, outs, got, terms, window_one, window_last)
+
+
+def step_one(both, inverse, part, rows):
+    cols = inverse.shape[2]
+
+    def one(both_ref, inverse_ref, out_ref):
+        value = (-summed(both_ref)).astype(BF16)
+        share = jnp.dot(value[:part], inverse_ref[1], preferred_element_type=F32)
+        link = lax.dot_general(
+            value[part:], inverse_ref[2], (((0,), (0,)), ((), ())),
+            preferred_element_type=F32,
+        )
+        for z in range(NUM_Z):
+            out_ref[z, :part, :] = share.astype(BF16)
+            out_ref[z, part:, :] = link[z * rows : (z + 1) * rows].astype(BF16)
+
+    return stage(one, [(NUM_Z, part + rows, cols)], both, inverse)[0]
+
+
 def fan(terms, solved, window):
     part, cols = terms.shape[0], solved.shape[1]
 
@@ -305,31 +380,14 @@
         packed, rows, part
     )
 
-    def over_narrow(value):
-        return total(spread(value.astype(BF16), NARROW, NUM_NARROW))
-
-    residue = (-over_narrow(first_terms[0])).astype(BF16)
-    share = jnp.dot(residue, inverse[0], preferred_element_type=F32).astype(BF16)
-    got = spread(jnp.concatenate([share, own]), "z", NUM_Z)
-    solved_0 = total(got[:, :part]).astype(BF16)
-    ahead = got[:, part:].reshape(NUM_Z * rows, cols)
-
-    fanned = first_terms[1] + lax.dot_general(
-        solved_0, window_one, ROWS_T, preferred_element_type=F32
-    )
-    link = lax.dot_general(window_last, ahead, ROWS_T, preferred_element_type=F32)
-    both = over_narrow(jnp.concatenate([fanned, link]))
-    residue, link = (-both[:part]).astype(BF16), (-both[part:]).astype(BF16)
-    share = jnp.dot(residue, inverse[1], preferred_element_type=F32).astype(BF16)
-    link = lax.dot_general(
-        link, inverse[2], (((0,), (0,)), ((), ())), preferred_element_type=F32
-    )
-    copies = jnp.broadcast_to(share[None], (NUM_Z,) + share.shape)
-    link = link.astype(BF16).reshape(NUM_Z, rows, cols)
-    got = lax.all_to_all(
-        jnp.concatenate([copies, link], axis=1), "z", 0, 0, tiled=True
-    )
-    got = total(got).astype(BF16)
+    fanned = spread(first_terms[0].astype(BF16), NARROW, NUM_NARROW)
+    got = step_zero(fanned, inverse, own)
+    got = lax.all_to_all(got, "z", 0, 0, tiled=True)
+
+    solved_0, both = step_one_fan(got, first_terms, window_one, window_last)
+    both = lax.all_to_all(both, NARROW, 0, 0, tiled=True)
+    got = step_one(both, inverse, part, rows)
+    got = total(lax.all_to_all(got, "z", 0, 0, tiled=True)).astype(BF16)
 
     stack = jnp.concatenate([solved_0, got, own])
     early = spread(stack, "y", NUM_Y)

time: 154 us -> 154 us (level)
    all_to_all x4 -> x2, blocking collectives: 61.2 us -> 30.3 us  [spread(): return lax.all_to_all(copies, axis, 0, 0, tiled=True)]
    all_to_all x1 -> x3, blocking collectives: 10.8 us -> 41.8 us  [the longest x1 17.9 us: per_device(): got = lax.all_to_all(got, 'z', 0, 0, tiled=True)]
where the time goes in v7:
time: 154 us; the launch traced here: 153 us
  blocking collectives  138 us (90%)
  starting transfers between devices  7.36 us (5%)
  Pallas kernels  5.17 us (3%)
    all_to_all x2, blocking collectives, spread(): return lax.all_to_all(copies, axis, 0, 0, tiled=True)  30.3 us
    all_to_all x1, blocking collectives, per_device(): packed = lax.all_to_all(packed, 'y', 0, 0, tiled=True)  18.9 us
    all_to_all x1, blocking collectives, per_device(): got = lax.all_to_all(got, 'z', 0, 0, tiled=True)  17.9 us
    all_to_all x1, blocking collectives, per_device(): trailing = total(lax.all_to_all(kept, 'x', 0, 0, tiled=True))  17.1 us
    all_gather x1, blocking collectives, per_device(): fanned = lax.all_gather(fan(late_terms, stack, window_two), NARROW, axis=0)  15 us
    all_to_all x1, blocking collectives, per_device(): late = total(lax.all_to_all(share, 'z', 0, 0, tiled=True)).astype(BF16)  14.8 us
    all_to_all x1, blocking collectives, per_device(): both = lax.all_to_all(both, NARROW, 0, 0, tiled=True)  13.1 us
    all_to_all x1, blocking collectives, per_device(): got = total(lax.all_to_all(got, 'z', 0, 0, tiled=True)).astype(BF16)  10.8 us
  transfers between devices with their start and end apart: 2, of which 1 were waited for; matrix products, arithmetic and copies ran while one was open for 0% of the time, Pallas kernels for 1%

profile of v7, /device:TPU:1, one launch (start us, length us, event | category | flops | bytes accessed | tf_op | source)
XLA Modules:
  0.0 153.3 jit_solution(2258835916770893851)
XLA Ops:
  0.6 1.1 pack.1
  1.8 18.9 %all_to_all.45.packed_ref = bf16[8,176,128]{2,1,0:T(8,128)(2,1)S(1)} all-to-all(bf16[8,176,128]{2,1,0:T(8,128)(2,1)S(1)} %get-tuple-element.12), channel_id=1, replica_groups=mesh['y'=8,'z'=8,'x'=4,'core'=2] {'y'}, dimensions={0} | all-to-all | bytes 720896 | tf_op jit(solution)/shard_map/all_to_all | solution.py:378
  20.8 12.8 %all_to_all.46.fanned_ref = bf16[8,64,128]{2,1,0:T(8,128)(2,1)S(1)} all-to-all(bf16[8,64,128]{2,1,0:T(8,128)(2,1)S(1)} %broadcast_in_dim.31), channel_id=1, replica_groups=mesh['y'=8,'z'=8,'x'=4,'core'=2] {'x','core'}, dimensions={0} | all-to-all | bytes 262144 | tf_op jit(solution)/shard_map/all_to_all | solution.py:29
  33.6 0.1 zero.1
  33.8 17.9 %all_to_all.47.got_ref = bf16[8,80,128]{2,1,0:T(8,128)(2,1)S(1)} all-to-all(bf16[8,80,128]{2,1,0:T(8,128)(2,1)S(1)} %zero.1), channel_id=1, replica_groups=mesh['y'=8,'z'=8,'x'=4,'core'=2] {'z'}, dimensions={0} | all-to-all | bytes 327680 | tf_op jit(solution)/shard_map/all_to_all | solution.py:385
  51.7 0.2 one_fan.1
  51.9 13.1 %all_to_all.48.both_ref = bf16[8,192,128]{2,1,0:T(8,128)(2,1)S(1)} all-to-all(bf16[8,192,128]{2,1,0:T(8,128)(2,1)S(1)} %get-tuple-element.19), channel_id=1, replica_groups=mesh['y'=8,'z'=8,'x'=4,'core'=2] {'x','core'}, dimensions={0} | all-to-all | bytes 786432 | tf_op jit(solution)/shard_map/all_to_all | solution.py:388
  64.9 0.2 one.1
  65.2 10.8 %all_to_all.49 = bf16[8,80,128]{2,1,0:T(8,128)(2,1)S(1)} all-to-all(bf16[8,80,128]{2,1,0:T(8,128)(2,1)S(1)} %one.1), channel_id=1, replica_groups=mesh['y'=8,'z'=8,'x'=4,'core'=2] {'z'}, dimensions={0} | all-to-all | bytes 327680 | tf_op jit(solution)/shard_map/all_to_all | solution.py:390
  76.0 0.8 broadcast_in_dim.32
  76.7 3.4 %all-to-all-start.5 = ((bf16[8,160,128]{2,1,0:T(8,128)(2,1)}), bf16[8,160,128]{2,1,0:T(8,128)(2,1)S(1)}, u32[]{:S(2)}, u32[]{:S(2)}) async-start(bf16[8,160,128]{2,1,0:T(8,128)(2,1)} %broadcast_in_dim.32), calls=%async_computation.5 | async-start | bytes 655360 | tf_op jit(solution)/shard_map/all_to_all | solution.py:29
  80.2 0.2 fan.1
  80.4 15.0 %all-gather = bf16[512,256]{1,0:T(8,128)(2,1)S(1)} all-gather(bf16[64,256]{1,0:T(8,128)(2,1)S(1)} %fan.1), channel_id=2, replica_groups=mesh['y'=8,'z'=8,'x'=4,'core'=2] {'x','core'}, dimensions={0}, use_global_device_ids=true | all-gather | bytes 294912 | tf_op jit(solution)/shard_map/all_gather | solution.py:394
  95.4 0.2 pair.1
  95.6 14.8 %all_to_all.50 = bf16[8,64,256]{2,1,0:T(8,128)(2,1)S(1)} all-to-all(bf16[8,64,256]{2,1,0:T(8,128)(2,1)S(1)} %pair.1), channel_id=1, replica_groups=mesh['y'=8,'z'=8,'x'=4,'core'=2] {'z'}, dimensions={0} | all-to-all | bytes 524288 | tf_op jit(solution)/shard_map/all_to_all | solution.py:396
  110.4 17.4 %all_to_all.51.late_ref = bf16[8,64,256]{2,1,0:T(8,128)(2,1)S(1)} all-to-all(bf16[8,64,256]{2,1,0:T(8,128)(2,1)S(1)} %broadcast_in_dim.33), channel_id=1, replica_groups=mesh['y'=8,'z'=8,'x'=4,'core'=2] {'y'}, dimensions={0} | all-to-all | bytes 524288 | tf_op jit(solution)/shard_map/all_to_all | solution.py:29
  127.9 0.9 product.3
  128.8 3.9 %collective-permute-start = (bf16[4,256,512]{2,1,0:T(8,128)(2,1)S(1)}, bf16[4,256,512]{2,1,0:T(8,128)(2,1)S(1)}, u32[]{:S(2)}, u32[]{:S(2)}) collective-permute-start(bf16[4,256,512]{2,1,0:T(8,128)(2,1)S(1)} %product.3), channel_id=1, source_target_pairs={{0,1},{1,0},{2,3},{3,2},{4,5},{5,4},{6,7},{7,6},{8,9},{9,8},{10,11... | collective-permute-start | bytes 3145736 | tf_op jit(solution)/shard_map/ppermute | solution.py:401
  132.7 1.0 turn.1._
  133.7 0.9 product.2.kept_ref
  134.6 0.4 collective-permute-done.back_ref
  135.0 0.3 merge.1
  135.3 17.1 %all_to_all.52 = bf16[4,256,512]{2,1,0:T(8,128)(2,1)S(1)} all-to-all(bf16[4,256,512]{2,1,0:T(8,128)(2,1)S(1)} %merge.1), channel_id=1, replica_groups=mesh['y'=8,'z'=8,'x'=4,'core'=2] {'x'}, dimensions={0} | all-to-all | bytes 2097152 | tf_op jit(solution)/shard_map/all_to_all | solution.py:405
  152.4 0.9 convert_reduce_fusion
  (10 shorter events, 0.2 us)
Async XLA Ops:
  76.0 51.9 %copy-start = (bf16[2048,4,128]{2,1,0:T(4,128)(2,1)S(1)}, bf16[2048,4,128]{2,1,0:T(4,128)(2,1)}, u32[]{:S(2)}) copy-start(bf16[2048,4,128]{2,1,0:T(4,128)(2,1)} %factor_ref.3) | copy-start | bytes 6291460
  76.7 18.6 %all-to-all-start.5 = ((bf16[8,160,128]{2,1,0:T(8,128)(2,1)}), bf16[8,160,128]{2,1,0:T(8,128)(2,1)S(1)}, u32[]{:S(2)}, u32[]{:S(2)}) async-start(bf16[8,160,128]{2,1,0:T(8,128)(2,1)} %broadcast_in_dim.32), calls=%async_computation.5 | async-start | bytes 655360 | tf_op jit(solution)/shard_map/all_to_all | solution.py:29
  128.8 6.2 %collective-permute-start = (bf16[4,256,512]{2,1,0:T(8,128)(2,1)S(1)}, bf16[4,256,512]{2,1,0:T(8,128)(2,1)S(1)}, u32[]{:S(2)}, u32[]{:S(2)}) collective-permute-start(bf16[4,256,512]{2,1,0:T(8,128)(2,1)S(1)} %product.3), channel_id=1, source_target_pairs={{0,1},{1,0},{2,3},{3,2},{4,5},{5,4},{6,7},{7,6},{8,9},{9,8},{10,11... | collective-permute-start | bytes 3145736 | tf_op jit(solution)/shard_map/ppermute | solution.py:401

commit v8 on v7

--- a/solution.py
+++ b/solution.py
@@ -380,12 +380,12 @@
         packed, rows, part
     )
 
-    fanned = spread(first_terms[0].astype(BF16), NARROW, NUM_NARROW)
+    fanned = spread(first_terms[0].astype(BF16), NARROW[::-1], NUM_NARROW)
     got = step_zero(fanned, inverse, own)
     got = lax.all_to_all(got, "z", 0, 0, tiled=True)
 
     solved_0, both = step_one_fan(got, first_terms, window_one, window_last)
-    both = lax.all_to_all(both, NARROW, 0, 0, tiled=True)
+    both = lax.all_to_all(both, NARROW[::-1], 0, 0, tiled=True)
     got = step_one(both, inverse, part, rows)
     got = total(lax.all_to_all(got, "z", 0, 0, tiled=True)).astype(BF16)
 

time: 154 us -> 154 us (level)
  no operation moved by 1% of the time
where the time goes in v8:
time: 154 us; the launch traced here: 153 us
  blocking collectives  138 us (90%)
  starting transfers between devices  7.36 us (5%)
  Pallas kernels  5.18 us (3%)
    all_to_all x2, blocking collectives, spread(): return lax.all_to_all(copies, axis, 0, 0, tiled=True)  30.2 us
    all_to_all x1, blocking collectives, per_device(): packed = lax.all_to_all(packed, 'y', 0, 0, tiled=True)  18.9 us
    all_to_all x1, blocking collectives, per_device(): got = lax.all_to_all(got, 'z', 0, 0, tiled=True)  18.5 us
    all_to_all x1, blocking collectives, per_device(): trailing = total(lax.all_to_all(kept, 'x', 0, 0, tiled=True))  17.1 us
    all_to_all x1, blocking collectives, per_device(): late = total(lax.all_to_all(share, 'z', 0, 0, tiled=True)).astype(BF16)  14.8 us
    all_gather x1, blocking collectives, per_device(): fanned = lax.all_gather(fan(late_terms, stack, window_two), NARROW, axis=0)  14.4 us
    all_to_all x1, blocking collectives, per_device(): both = lax.all_to_all(both, NARROW[::-1], 0, 0, tiled=True)  12.5 us
    all_to_all x1, blocking collectives, per_device(): got = total(lax.all_to_all(got, 'z', 0, 0, tiled=True)).astype(BF16)  11.4 us
  transfers between devices with their start and end apart: 2, of which 1 were waited for; matrix products, arithmetic and copies ran while one was open for 0% of the time, Pallas kernels for 1%

profile of v8, /device:TPU:1, one launch (start us, length us, event | category | flops | bytes accessed | tf_op | source)
XLA Modules:
  0.0 153.2 jit_solution(5226654293609355356)
XLA Ops:
  0.6 1.1 pack.1
  1.8 18.9 %all_to_all.45.packed_ref = bf16[8,176,128]{2,1,0:T(8,128)(2,1)S(1)} all-to-all(bf16[8,176,128]{2,1,0:T(8,128)(2,1)S(1)} %get-tuple-element.12), channel_id=1, replica_groups=mesh['y'=8,'z'=8,'x'=4,'core'=2] {'y'}, dimensions={0} | all-to-all | bytes 720896 | tf_op jit(solution)/shard_map/all_to_all | solution.py:378
  20.8 12.8 %all_to_all.46.fanned_ref = bf16[8,64,128]{2,1,0:T(8,128)(2,1)S(1)} all-to-all(bf16[8,64,128]{2,1,0:T(8,128)(2,1)S(1)} %broadcast_in_dim.31), channel_id=1, replica_groups=mesh['y'=8,'z'=8,'x'=4,'core'=2] {'core','x'}, dimensions={0} | all-to-all | bytes 262144 | tf_op jit(solution)/shard_map/all_to_all | solution.py:29
  33.6 0.1 zero.1
  33.7 18.5 %all_to_all.47.got_ref = bf16[8,80,128]{2,1,0:T(8,128)(2,1)S(1)} all-to-all(bf16[8,80,128]{2,1,0:T(8,128)(2,1)S(1)} %zero.1), channel_id=1, replica_groups=mesh['y'=8,'z'=8,'x'=4,'core'=2] {'z'}, dimensions={0} | all-to-all | bytes 327680 | tf_op jit(solution)/shard_map/all_to_all | solution.py:385
  52.2 0.2 one_fan.1
  52.4 12.5 %all_to_all.48.both_ref = bf16[8,192,128]{2,1,0:T(8,128)(2,1)S(1)} all-to-all(bf16[8,192,128]{2,1,0:T(8,128)(2,1)S(1)} %get-tuple-element.19), channel_id=1, replica_groups=mesh['y'=8,'z'=8,'x'=4,'core'=2] {'core','x'}, dimensions={0} | all-to-all | bytes 786432 | tf_op jit(solution)/shard_map/all_to_all | solution.py:388
  64.8 0.2 one.1
  65.1 11.4 %all_to_all.49 = bf16[8,80,128]{2,1,0:T(8,128)(2,1)S(1)} all-to-all(bf16[8,80,128]{2,1,0:T(8,128)(2,1)S(1)} %one.1), channel_id=1, replica_groups=mesh['y'=8,'z'=8,'x'=4,'core'=2] {'z'}, dimensions={0} | all-to-all | bytes 327680 | tf_op jit(solution)/shard_map/all_to_all | solution.py:390
  76.5 0.8 broadcast_in_dim.32
  77.3 3.4 %all-to-all-start.5 = ((bf16[8,160,128]{2,1,0:T(8,128)(2,1)}), bf16[8,160,128]{2,1,0:T(8,128)(2,1)S(1)}, u32[]{:S(2)}, u32[]{:S(2)}) async-start(bf16[8,160,128]{2,1,0:T(8,128)(2,1)} %broadcast_in_dim.32), calls=%async_computation.5 | async-start | bytes 655360 | tf_op jit(solution)/shard_map/all_to_all | solution.py:29
  80.8 0.2 fan.1
  80.9 14.4 %all-gather = bf16[512,256]{1,0:T(8,128)(2,1)S(1)} all-gather(bf16[64,256]{1,0:T(8,128)(2,1)S(1)} %fan.1), channel_id=2, replica_groups=mesh['y'=8,'z'=8,'x'=4,'core'=2] {'x','core'}, dimensions={0}, use_global_device_ids=true | all-gather | bytes 294912 | tf_op jit(solution)/shard_map/all_gather | solution.py:394
  95.3 0.2 pair.1
  95.5 14.8 %all_to_all.50 = bf16[8,64,256]{2,1,0:T(8,128)(2,1)S(1)} all-to-all(bf16[8,64,256]{2,1,0:T(8,128)(2,1)S(1)} %pair.1), channel_id=1, replica_groups=mesh['y'=8,'z'=8,'x'=4,'core'=2] {'z'}, dimensions={0} | all-to-all | bytes 524288 | tf_op jit(solution)/shard_map/all_to_all | solution.py:396
  110.3 17.4 %all_to_all.51.late_ref = bf16[8,64,256]{2,1,0:T(8,128)(2,1)S(1)} all-to-all(bf16[8,64,256]{2,1,0:T(8,128)(2,1)S(1)} %broadcast_in_dim.33), channel_id=1, replica_groups=mesh['y'=8,'z'=8,'x'=4,'core'=2] {'y'}, dimensions={0} | all-to-all | bytes 524288 | tf_op jit(solution)/shard_map/all_to_all | solution.py:29
  127.8 0.9 product.3
  128.7 3.9 %collective-permute-start = (bf16[4,256,512]{2,1,0:T(8,128)(2,1)S(1)}, bf16[4,256,512]{2,1,0:T(8,128)(2,1)S(1)}, u32[]{:S(2)}, u32[]{:S(2)}) collective-permute-start(bf16[4,256,512]{2,1,0:T(8,128)(2,1)S(1)} %product.3), channel_id=1, source_target_pairs={{0,1},{1,0},{2,3},{3,2},{4,5},{5,4},{6,7},{7,6},{8,9},{9,8},{10,11... | collective-permute-start | bytes 3145736 | tf_op jit(solution)/shard_map/ppermute | solution.py:401
  132.6 1.0 turn.1._
  133.6 0.9 product.2.kept_ref
  134.5 0.4 collective-permute-done.back_ref
  134.9 0.3 merge.1
  135.2 17.1 %all_to_all.52 = bf16[4,256,512]{2,1,0:T(8,128)(2,1)S(1)} all-to-all(bf16[4,256,512]{2,1,0:T(8,128)(2,1)S(1)} %merge.1), channel_id=1, replica_groups=mesh['y'=8,'z'=8,'x'=4,'core'=2] {'x'}, dimensions={0} | all-to-all | bytes 2097152 | tf_op jit(solution)/shard_map/all_to_all | solution.py:405
  152.3 0.9 convert_reduce_fusion
  (10 shorter events, 0.2 us)
Async XLA Ops:
  76.5 51.2 %copy-start = (bf16[2048,4,128]{2,1,0:T(4,128)(2,1)S(1)}, bf16[2048,4,128]{2,1,0:T(4,128)(2,1)}, u32[]{:S(2)}) copy-start(bf16[2048,4,128]{2,1,0:T(4,128)(2,1)} %factor_ref.3) | copy-start | bytes 6291460
  77.3 18.0 %all-to-all-start.5 = ((bf16[8,160,128]{2,1,0:T(8,128)(2,1)}), bf16[8,160,128]{2,1,0:T(8,128)(2,1)S(1)}, u32[]{:S(2)}, u32[]{:S(2)}) async-start(bf16[8,160,128]{2,1,0:T(8,128)(2,1)} %broadcast_in_dim.32), calls=%async_computation.5 | async-start | bytes 655360 | tf_op jit(solution)/shard_map/all_to_all | solution.py:29
  128.7 6.2 %collective-permute-start = (bf16[4,256,512]{2,1,0:T(8,128)(2,1)S(1)}, bf16[4,256,512]{2,1,0:T(8,128)(2,1)S(1)}, u32[]{:S(2)}, u32[]{:S(2)}) collective-permute-start(bf16[4,256,512]{2,1,0:T(8,128)(2,1)S(1)} %product.3), channel_id=1, source_target_pairs={{0,1},{1,0},{2,3},{3,2},{4,5},{5,4},{6,7},{7,6},{8,9},{9,8},{10,11... | collective-permute-start | bytes 3145736 | tf_op jit(solution)/shard_map/ppermute | solution.py:401
